TPU v7x, 512 devices: a whole 4x4x16 slice. The times are simulated.
512 devices in a mesh: grp: 16 (over z), dev: 32 (over y, x, core).
Axes of the slice: x: 4, y: 4, z: 16, core: 2. Of those that a mesh axis runs over, the one named last changes fastest.
Arguments:
- particles: bfloat16 [8192, 2, 6144], P(('grp', 'dev')), may hold values from -24 to 24
- defocus_bin: int32 [8192], P(('grp', 'dev')), may hold values from 0 to 15
- candidates: int32 [8192, 8], P(('grp', 'dev')), may hold values from 0 to 63, as said below
- projections: bfloat16 [64, 2, 6144], P('dev'), may hold values from -1 to 1
- ctf_table: bfloat16 [16, 6144], replicated, may hold values from -1 to 1
- inv_noise: float32 [6144], replicated, may hold values from 0.25 to 4
- line_slab: int32 [64, 48], P('dev'), may hold values from 0 to 15, as said below
- slab_owner: int32 [16], replicated, may hold values from 0 to 15, each once
Outputs:
- slab_data: float32 [16, 64, 2, 6, 128], P('grp', 'dev')
- slab_weight: float32 [16, 64, 6, 128], P('grp', 'dev')
Inputs may be any that keep to these rules, and one draw needn't show every extreme that they name: `candidates`: each particle lists 8 different projections. `line_slab`: no slab holds more than 6 lines of one projection, and for every projection one slab holds exactly 6 of them. `slab_owner`: each group owns exactly one slab.
All inputs are finite; a program needn't handle non-finite values.
Results may differ from a plain program's by a relative error of at most 0.02.
Values may be sent and summed in bfloat16 or wider, within the bound.
A program may use at most 64 MiB of HBM per device.

v0:
```python
import math

import jax
import jax.numpy as jnp
from jax import lax
from jax.sharding import PartitionSpec as P

LINE_LEN = 128
PIXELS = 6144
SHIFTS = 9


two_pi = 2.0 * math.pi
exact = lax.Precision.HIGHEST
contract_rows = (((0,), (0,)), ((), ()))
contract_last = (((1,), (1,)), ((), ()))


def phase_tables():
    pixel_index = jnp.arange(PIXELS, dtype=jnp.int32)
    line_pos = (pixel_index // LINE_LEN).astype(jnp.float32)
    column = pixel_index % LINE_LEN
    frequency = jnp.where(column < LINE_LEN // 2, column, column - LINE_LEN).astype(jnp.float32)
    shift_index = jnp.arange(SHIFTS, dtype=jnp.int32)
    move_x = (shift_index // 3 - 1).astype(jnp.float32)
    move_y = (shift_index % 3 - 1).astype(jnp.float32)
    angles = (move_x[:, None] * line_pos[None, :] + move_y[:, None] * frequency[None, :]) * (
        two_pi / LINE_LEN
    )
    return (jnp.cos(angles), jnp.sin(angles))


def slot_tables(line_slab, slab_owner, groups):
    group_ids = jnp.arange(groups, dtype=jnp.int32)
    slab_hit = line_slab[:, :, None] == group_ids[None, None, :]
    owner_line = jnp.sum(jnp.where(slab_hit, slab_owner[None, None, :], 0), axis=2)
    line_ids = jnp.arange(line_slab.shape[1], dtype=jnp.int32)
    earlier = line_ids[None, :] < line_ids[:, None]
    same_owner = owner_line[:, :, None] == owner_line[:, None, :]
    line_rank = jnp.sum(jnp.logical_and(same_owner, earlier[None]), axis=2)
    return (owner_line, line_rank)


def route_lines(values, owner_line, line_rank, groups, capacity):
    group_ids = jnp.arange(groups, dtype=jnp.int32)
    slot_ids = jnp.arange(capacity, dtype=jnp.int32)
    selector = jnp.logical_and(
        owner_line[:, None, None, :] == group_ids[None, :, None, None],
        line_rank[:, None, None, :] == slot_ids[None, None, :, None],
    ).astype(jnp.float32)
    packed = jnp.einsum("jocl,jxlp->ojxcp", selector, values, precision=exact)
    return lax.psum_scatter(
        packed.astype(jnp.bfloat16), "grp", scatter_dimension=0, tiled=True
    ).astype(jnp.float32)[0]


def body(
    particles, defocus_bin, candidates, projections, ctf_table, inv_noise, line_slab, slab_owner
):
    part_dev = particles.shape[0]
    pixels = particles.shape[2]
    proj_dev = projections.shape[0]
    groups = lax.axis_size("grp")
    members = lax.axis_size("dev")
    proj_all = proj_dev * members
    line_count = line_slab.shape[1]
    line_len = pixels // line_count
    capacity = 2 * line_count // groups
    cosines, sine_table = phase_tables()
    table_values = ctf_table.astype(jnp.float32)
    ctf_square = table_values * table_values
    noisy_square = ctf_square * inv_noise[None, :]
    onehot = (
        defocus_bin[:, None] == jnp.arange(ctf_table.shape[0], dtype=jnp.int32)[None, :]
    ).astype(jnp.float32)
    ctf_rows = jnp.dot(onehot, table_values, precision=exact)
    weighted = (
        ((inv_noise[None, :] * ctf_rows)[:, None, :] * particles)
        .astype(jnp.bfloat16)
        .reshape(part_dev, 2 * pixels)
    )
    ctf_image = (
        (ctf_rows[:, None, :] * particles).astype(jnp.bfloat16).reshape(part_dev, 2 * pixels)
    )
    values = lax.all_gather(projections, "dev", axis=0, tiled=True).astype(jnp.float32)
    pix_power = values[:, 0] * values[:, 0] + values[:, 1] * values[:, 1]
    bin_power = lax.dot_general(noisy_square, pix_power, contract_last, precision=exact)
    quad_term = jnp.dot(onehot, bin_power, precision=exact)

    def one_shift(tables):
        cos_row, sin_row = tables
        real_part = values[:, 0] * cos_row[None, :] - values[:, 1] * sin_row[None, :]
        imag_part = values[:, 0] * sin_row[None, :] + values[:, 1] * cos_row[None, :]
        rotated = jnp.concatenate([real_part, imag_part], axis=1).astype(jnp.bfloat16)
        return lax.dot_general(weighted, rotated, contract_last, preferred_element_type=jnp.float32)

    scored = lax.map(one_shift, (cosines, sine_table))
    scores = jnp.transpose(scored, (1, 0, 2)) - 0.5 * quad_term[:, None, :]
    proj_ids = jnp.arange(proj_all, dtype=jnp.int32)
    listed = jnp.any(candidates[:, :, None] == proj_ids[None, None, :], axis=1)
    masked = jnp.where(listed[:, None, :], scores, -jnp.inf)
    row_peak = jnp.max(masked, axis=(1, 2), keepdims=True)
    exp_terms = jnp.exp(masked - row_peak)
    posterior = exp_terms / jnp.sum(exp_terms, axis=(1, 2), keepdims=True)
    by_shift = jnp.transpose(posterior.astype(jnp.bfloat16), (1, 0, 2))

    def add_shift(running, inputs):
        weights_now, cos_row, sin_row = inputs
        summed = lax.dot_general(
            weights_now, ctf_image, contract_rows, preferred_element_type=jnp.float32
        )
        real_sum = summed[:, :pixels]
        imag_sum = summed[:, pixels:]
        turned = jnp.stack(
            [
                real_sum * cos_row[None, :] + imag_sum * sin_row[None, :],
                imag_sum * cos_row[None, :] - real_sum * sin_row[None, :],
            ],
            axis=1,
        )
        return (running + turned, None)

    start_sum = jnp.zeros((proj_dev * lax.axis_size("dev"), 2, pixels), jnp.float32)
    result, _ = lax.scan(add_shift, start_sum, (by_shift, cosines, sine_table))
    data_part = lax.psum_scatter(
        result.astype(jnp.bfloat16), "dev", scatter_dimension=0, tiled=True
    ).astype(jnp.float32)
    proj_share = jnp.sum(posterior, axis=1)
    weight_scale = proj_all / (part_dev * groups * members)
    owner_line, line_rank = slot_tables(line_slab, slab_owner, groups)
    data_lines = data_part.reshape(proj_dev, 2, line_count, line_len)
    ctf_rows_sq = ctf_rows * ctf_rows
    weight_part = (
        lax.psum_scatter(
            lax.dot_general(
                proj_share,
                ctf_rows_sq,
                contract_rows,
                precision=exact,
                preferred_element_type=jnp.float32,
            ).astype(jnp.bfloat16),
            "dev",
            scatter_dimension=0,
            tiled=True,
        ).astype(jnp.float32)
        * weight_scale
    )
    stacked = jnp.concatenate(
        [data_lines, weight_part.reshape(proj_dev, 1, line_count, line_len)], axis=1
    )
    routed = route_lines(stacked, owner_line, line_rank, groups, capacity)
    return (routed[None, :, :2], routed[None, :, 2])


def solution(mesh):
    return jax.shard_map(
        body,
        mesh=mesh,
        in_specs=(
            P(("grp", "dev"), None, None),
            P(("grp", "dev")),
            P(("grp", "dev"), None),
            P("dev", None, None),
            P(),
            P(),
            P("dev", None),
            P(),
        ),
        out_specs=(P("grp", "dev", None, None, None), P("grp", "dev", None, None)),
        check_vma=False,
    )
```

profile of v0, /device:TPU:4, one launch (start us, length us, event | category | flops | bytes accessed | tf_op | source)
XLA Modules:
  0.0 495.3 jit_solution(7120821625978491027)
XLA Ops:
  9.2 1.8 fusion.25
  12.2 2.4 fusion.30
  14.6 59.1 %all-gather.2.cloned.1.call-done = bf16[64,2,6144]{2,1,0:T(2,128)(2,1)} async-done(((bf16[2,2,6144]{2,1,0:T(2,128)(2,1)}), bf16[64,2,6144]{2,1,0:T(2,128)(2,1)}) %all-gather.2.cloned.1.call-update) | async-done | bytes 1572880 | tf_op jit(solution)/shard_map/all_gather | solution.py:85
  73.7 3.2 convert_element_type.95
  76.9 3.0 fusion.19
  79.9 59.7 %while.21 = (s32[]{:T(128)}, f32[9,16,64]{2,1,0:T(8,128)}, f32[64,2,6144]{2,1,0:T(2,128)S(1)}, f32[9,6144]{1,0:T(8,128)}, f32[9,6144]{1,0:T(8,128)}, /*index=5*/bf16[16,12288]{1,0:T(8,128)(2,1)}, s32[]{:T(128)}) while((s32[]{:T(128)}, f32[9,16,64]{2,1,0:T(8,128)}, f32[64,2,6144]{2,1,0:T(2,128)S(1)}, f32[9,6144]{1,0:T(8,128)}, ...), condition=%wide.region_2.3_spmd, body=%wide.region_1.2_spmd.sunk | while | flops 31457280 | bytes 17850988 | solution.py:97
  81.0 1.8 copy.56
  82.8 1.6 slice.63
  87.6 1.8 copy.56
  89.4 1.6 slice.63
  94.2 1.8 copy.56
  96.1 1.6 slice.63
  100.9 1.8 copy.56
  102.7 1.6 slice.63
  107.5 1.8 copy.56
  109.3 1.6 slice.63
  114.1 1.8 copy.56
  116.0 1.6 slice.63
  120.8 1.8 copy.56
  122.6 1.6 slice.63
  127.4 1.8 copy.56
  129.2 1.6 slice.63
  134.1 1.8 copy.56
  135.9 1.6 slice.63
  139.6 3.1 fusion.20
  145.0 1.6 fusion.61
  146.6 57.7 %while.22 = (s32[]{:T(128)}, f32[64,2,6144]{2,0,1:T(8,128)}, bf16[9,16,64]{2,1,0:T(8,128)(2,1)}, bf16[16,12288]{1,0:T(8,128)(2,1)S(1)}, f32[9,6144]{1,0:T(8,128)}, /*index=5*/f32[9,6144]{1,0:T(8,128)}, s32[]{:T(128)}, s32[]{:T(128)}) while((s32[]{:T(128)}, f32[64,2,6144]{2,0,1:T(8,128)}, bf16[9,16,64]{2,1,0:T(8,128)(2,1)}, ...), condition=%wide.region_6.7_spmd.clone, body=%wide.region_5.6_spmd.clone.sunk | while | flops 29884416 | bytes 19419748 | solution.py:124
  147.7 1.3 fusion.82
  149.4 2.0 maximum_add_fusion.2
  154.1 3.9 maximum_add_fusion.2
  159.0 1.3 fusion.82
  160.7 3.9 maximum_add_fusion.2
  167.4 3.9 maximum_add_fusion.2
  172.3 1.3 fusion.82
  174.0 3.9 maximum_add_fusion.2
  178.9 1.3 fusion.82
  180.6 3.9 maximum_add_fusion.2
  187.2 3.9 maximum_add_fusion.2
  193.8 3.9 maximum_add_fusion.2
  198.8 1.3 fusion.82
  200.5 3.9 maximum_add_fusion.2
  204.3 3.3 convert_element_type.105
  207.7 2.3 convolution_convert_fusion
  210.1 1.3 dynamic-slice
  212.3 135.5 %all-reduce.9.cloned.1.call-done = (bf16[64,6144]{1,0:T(8,128)(2,1)}, bf16[64,2,6144]{2,0,1:T(8,128)(2,1)}) async-done(((bf16[64,6144]{1,0:T(8,128)(2,1)}, bf16[64,2,6144]{2,0,1:T(8,128)(2,1)}), (bf16[64,6144]{1,0:T(8,128)(2,1)}, bf16[64,2,6144]{2,0,1:T(8,128)(2,1)})) %all-reduce.9.cloned.1.call-update) | async-done | bytes 2359312
  350.9 1.3 dynamic-slice.4
  352.2 134.0 %all-reduce.7.cloned.1.call-done = bf16[16,2,3,6,128]{4,1,3,2,0:T(2,128)(2,1)} async-done(((bf16[16,2,3,6,128]{4,1,3,2,0:T(2,128)(2,1)}), bf16[16,2,3,6,128]{4,1,3,2,0:T(2,128)(2,1)}) %all-reduce.7.cloned.1.call-update) | async-done | bytes 147472
  486.2 1.4 fusion.52
  (114 shorter events, 56.8 us)
Async XLA Ops:
  7.2 66.6 %all-gather.2.cloned.1.call-start = ((), (), s32[]{:S(2)}) async-start(), calls=%async_computation | async-start | bytes 1622016 | tf_op jit(solution)/shard_map/all_gather | solution.py:85
  7.9 339.9 %all-reduce.9.cloned.1.call-start = ((), (), s32[]{:S(2)}) async-start(), calls=%async_computation.2 | async-start | bytes 4718592
  9.2 2.8 copy-start
  9.2 2.7 copy-start.4
  84.4 1.0 copy-start.2
  91.1 1.0 copy-start.2
  97.7 1.0 copy-start.2
  104.3 1.0 copy-start.2
  111.0 1.0 copy-start.2
  117.6 1.0 copy-start.2
  124.2 1.0 copy-start.2
  130.9 1.0 copy-start.2
  137.5 1.0 copy-start.2
  139.6 3.1 copy-start.6
  204.3 3.3 copy-start.3
  204.3 3.3 copy-start.1
  207.6 4.4 copy-start.5
  207.6 4.4 copy-start.7
  210.0 276.2 %all-reduce.7.cloned.1.call-start = ((), (), s32[]{:S(2)}) async-start(), calls=%async_computation.1 | async-start | bytes 294912
Sparse Core Ops, SparseCore 0:
  11.1 62.5 all-gather.1
  210.1 137.6 all-reduce.8
  351.0 135.1 all-reduce.6
where the time goes:
time: 497 us; the launch traced here: 495 us
  waiting for transfers between devices  329 us (66%)
  other arithmetic  63.9 us (13%)
  local copies, waits for them, and re-layouts  58.4 us (12%)
  matrix products  28.5 us (6%)
  between operations  14.6 us (3%)
    unnamed x5, waiting for transfers between devices  270 us
    all_gather x1, waiting for transfers between devices, body(): lax.all_gather(projections, 'dev', axis=0, tiled=True).astype(jnp.float32)  59.1 us
    add x9, other arithmetic, add_shift(): return (running + turned, None)  32.9 us
    dynamic_slice x18, local copies, waits for them, and re-layouts, body(): scored = lax.map(one_shift, (cosines, sine_table))  19 us
    another operation x9, local copies, waits for them, and re-layouts  16.4 us
    slice x9, local copies, waits for them, and re-layouts, one_shift(): values[:, 1] * sin_row[None, :]  14.6 us
    dot_general x9, matrix products, add_shift(): lax.dot_general(weights_now, ctf_image, contract_rows, preferred_element_...  11.4 us
    dot_general x9, matrix products, one_shift(): lax.dot_general(weighted, rotated, contract_last, preferred_element_type=...  10.1 us
  transfers between devices with their start and end apart: 3, of which 3 were waited for; matrix products, arithmetic and copies ran while one was open for 2% of the time, Pallas kernels for 0%

commit v1 on v0

v1 whole, which is shorter than its diff:
```python
import math

import jax
import jax.numpy as jnp
import numpy as np
from jax import lax
from jax.experimental import pallas as pl
from jax.experimental.pallas import tpu as pltpu
from jax.sharding import PartitionSpec as P

LINE = 128
CAP = 6
BINS = 16
NODES = 16
COLOURS = 4
ROWS = 8
NEG = -3.0e38
MESH = pl.DeviceIdType.MESH
F32 = jnp.float32
BF16 = jnp.bfloat16
HIGH = lax.Precision.HIGHEST
NN = (((1,), (0,)), ((), ()))
NT = (((1,), (1,)), ((), ()))
TN = (((0,), (0,)), ((), ()))
STEPS = (1, 3, 4, 12)


def dot(a, b, dims=NN, precision=None):
    return lax.dot_general(a, b, dims, preferred_element_type=F32, precision=precision)


def phase_rows(lines):
    line = np.repeat(np.arange(lines), LINE).astype(np.float64)
    column = np.tile(np.arange(LINE), lines)
    freq = np.where(column < LINE // 2, column, column - LINE).astype(np.float64)
    moves = ((0, 1), (1, -1), (1, 0), (1, 1))
    angle = np.stack([dx * line + dy * freq for dx, dy in moves]) * (2.0 * math.pi / LINE)
    return np.concatenate([np.cos(angle), np.sin(angle)]).astype(np.float32)


def offset_of(colour, mask):
    off = 0
    for p in range(4):
        if mask >> p & 1:
            off ^= STEPS[(p + colour) % 4]
    return off


def flip(v, k):
    if k == 0:
        return v
    if k == 1:
        return v + 1 - 2 * (v % 2)
    if k == 2:
        return (v + 2) % 4
    return 3 - v


def top(mask):
    return mask.bit_length() - 1


def make_kernel(lines, groups):
    half = lines * LINE // 2
    width = half // COLOURS
    hl = lines // 2
    slots = 32

    def kernel(parts, proj, table, noise, trig, cand, bins, slab, owner,
               o_data, o_weight,
               xin, pin, candb, binb, trigv, tabh, tabf, noisev, asm, pbuf, rbuf, gscr, bpscr, sx,
               cscr, bsscr, dbuf, rsb, zb, sel, wkey, w3, zsend, zrecv, wzs, wzr,
               loc, ex_s, ex_r, ag_s, ag_r, rs_s, rs_r, sx_sem, zx_sem, z_s, z_r, w_s, w_r):
        z = lax.axis_index("grp")
        d = lax.axis_index("dev")
        core = d % 2
        node = d // 2
        nx, ny = node % 4, node // 4
        other = 1 - core

        def at(k):
            return flip(ny, k // 4) * 4 + flip(nx, k % 4)

        def dev(k):
            return (z, at(k) * 2 + core)

        mate = (z, node * 2 + other)

        barrier = pltpu.get_barrier_semaphore()
        pl.semaphore_signal(barrier, inc=1, device_id=mate, device_id_type=MESH)
        for k in STEPS:
            pl.semaphore_signal(barrier, inc=1, device_id=dev(k), device_id_type=MESH)
        for k in range(1, groups):
            pl.semaphore_signal(barrier, inc=1, device_id=((z + k) % groups, d), device_id_type=MESH)

        mine = pl.ds(pl.multiple_of(core * half, LINE), half)
        theirs = pl.ds(pl.multiple_of(other * half, LINE), half)
        loads = [
            pltpu.make_async_copy(proj.at[:, :, mine], pin.at[core], loc.at[0]),
            pltpu.make_async_copy(parts.at[:, :, mine], xin.at[core], loc.at[1]),
            pltpu.make_async_copy(table.at[:, mine], tabh, loc.at[2]),
            pltpu.make_async_copy(trig.at[:, mine], trigv, loc.at[3]),
            pltpu.make_async_copy(noise.at[:, mine], noisev, loc.at[4]),
            pltpu.make_async_copy(table, tabf, loc.at[5]),
            pltpu.make_async_copy(cand, candb.at[core], loc.at[6]),
            pltpu.make_async_copy(bins, binb.at[core], loc.at[7]),
        ]
        for c in loads:
            c.start()

        lanes = lax.broadcasted_iota(jnp.int32, (1, 128), 1)
        lid = lax.broadcasted_iota(jnp.int32, (groups, lines), 0)
        tri = (
            lax.broadcasted_iota(jnp.int32, (lines, lines), 0)
            < lax.broadcasted_iota(jnp.int32, (lines, lines), 1)
        ).astype(F32)
        wide = (
            lax.broadcasted_iota(jnp.int32, (lines, lines * ROWS), 1) // ROWS
            == lax.broadcasted_iota(jnp.int32, (lines, lines * ROWS), 0)
        ).astype(F32)
        wide16 = (
            lax.broadcasted_iota(jnp.int32, (lines, lines * BINS), 1) // BINS
            == lax.broadcasted_iota(jnp.int32, (lines, lines * BINS), 0)
        ).astype(F32)
        keys = []
        for j in range(2):
            row = slab[j : j + 1, :]
            own = jnp.zeros((1, lines), jnp.int32)
            for s in range(groups):
                own = own + jnp.where(row == s, owner[s], 0)
            hit = (lid == own).astype(F32)
            rank = jnp.sum(hit * dot(hit, tri), axis=0, keepdims=True)
            keys.append((own * 8).astype(F32) + rank)
        key8 = [dot(k, wide) for k in keys]
        col = lax.broadcasted_iota(jnp.int32, (1, lines * ROWS), 1) % ROWS
        pick = jnp.where(col % 4 >= 2, key8[1], key8[0]).astype(jnp.int32) * 8 + col
        rid = lax.broadcasted_iota(jnp.int32, (groups * slots, lines * ROWS), 0)
        inner = rid % slots
        r4 = (
            (inner >= CAP).astype(jnp.int32)
            + (inner >= 2 * CAP).astype(jnp.int32)
            + (inner >= 3 * CAP).astype(jnp.int32)
            + (inner >= 4 * CAP).astype(jnp.int32)
        )
        want = ((rid // slots) * 8 + (inner - CAP * r4)) * 8 + 4 * core + r4
        sel[...] = (want == pick).astype(F32).astype(BF16)
        for j in range(2):
            wkey[8 * j : 8 * j + 8, :] = jnp.broadcast_to(dot(keys[j], wide16), (8, lines * BINS))

        loads[2].wait()
        loads[3].wait()
        loads[1].wait()
        loads[7].wait()
        bid = lax.broadcasted_iota(jnp.int32, (BINS, 16), 0)

        def rotate(s):
            hot = (bid == binb[s]).astype(F32).astype(BF16)

            def chunk(i, carry):
                at_ = pl.ds(pl.multiple_of(i * width, LINE), width)
                ctf = dot(hot, tabh[:, at_], TN)
                for part in range(2):
                    x = ctf * xin[s, part, :, at_].astype(F32)
                    r0 = pl.multiple_of(512 + part * 32 + s * 16, 16)
                    rbuf[pl.ds(r0, 16), at_] = x.astype(BF16)
                    for u in range(8):
                        r0 = pl.multiple_of(part * 256 + u * 32 + s * 16, 16)
                        rbuf[pl.ds(r0, 16), at_] = (x * trigv[u : u + 1, at_]).astype(BF16)
                return carry

            lax.fori_loop(0, COLOURS, chunk, 0)

        rotate(core)
        for i in (0, 4, 5, 6):
            loads[i].wait()

        pl.semaphore_wait(barrier, 5 + groups - 1)

        swaps = []
        for i, (src, dst) in enumerate(
            (
                (proj.at[:, :, theirs], pin.at[core]),
                (parts.at[:, :, theirs], xin.at[core]),
                (cand, candb.at[core]),
                (bins, binb.at[core]),
            )
        ):
            swaps.append(
                pltpu.make_async_remote_copy(
                    src_ref=src, dst_ref=dst,
                    send_sem=ex_s.at[i], recv_sem=ex_r.at[i], device_id=mate, device_id_type=MESH,
                )
            )
        for c in swaps:
            c.start()
        swaps[0].wait_recv()
        for s in range(2):
            for j in range(2):
                asm[4 * s + 2 * j : 4 * s + 2 * j + 2, :] = pin[s, j].astype(F32)
        pbuf[node] = asm[...].astype(BF16)

        def span(q):
            return slice(q * width, (q + 1) * width)

        def ag(q, e, p):
            to = e | 1 << p
            m = at(offset_of(q, e))
            return pltpu.make_async_remote_copy(
                src_ref=pbuf.at[m, :, span(q)], dst_ref=pbuf.at[m, :, span(q)],
                send_sem=ag_s.at[q, to], recv_sem=ag_r.at[q, to],
                device_id=dev(STEPS[(p + q) % 4]), device_id_type=MESH,
            )

        def ag_in(q, e):
            m = at(offset_of(q, e))
            return pltpu.make_async_remote_copy(
                src_ref=pbuf.at[m, :, span(q)], dst_ref=pbuf.at[m, :, span(q)],
                send_sem=ag_s.at[q, e], recv_sem=ag_r.at[q, e],
                device_id=dev(STEPS[(top(e) + q) % 4]), device_id_type=MESH,
            )

        sent = []

        def push(c):
            c.start()
            sent.append(c)

        for p in range(4):
            for q in range(COLOURS):
                push(ag(q, 0, p))
        for e in (1,):
            for q in range(COLOURS):
                ag_in(q, e).wait_recv()
                for p in range(1, 4):
                    push(ag(q, e, p))
        for e in (2, 3):
            for q in range(COLOURS):
                ag_in(q, e).wait_recv()
                for p in range(2, 4):
                    push(ag(q, e, p))
        for e in (4, 5, 6, 7):
            for q in range(COLOURS):
                ag_in(q, e).wait_recv()
                push(ag(q, e, 3))

        swaps[1].wait_recv()
        swaps[2].wait_recv()
        swaps[3].wait_recv()
        rotate(other)

        ohb = jnp.zeros((128, 128), F32)
        cid = lax.broadcasted_iota(jnp.int32, (128, 128), 0)
        lane_core = (lanes % 32) // 16
        til = (
            lax.broadcasted_iota(jnp.int32, (16, 128), 1) % 16
            == lax.broadcasted_iota(jnp.int32, (16, 128), 0)
        ).astype(F32)
        bl = [dot(binb[s].astype(F32), til) for s in range(2)]
        blane = jnp.where(lane_core == 1, bl[1], bl[0]).astype(jnp.int32)
        ohb = (cid == blane).astype(F32)
        cl = [dot(candb[s].astype(F32), til, TN) for s in range(2)]
        clane = jnp.where(lane_core == 1, cl[1], cl[0]).astype(jnp.int32)
        jid = lax.broadcasted_iota(jnp.int32, (64, 128), 0)
        listed = jid == clane[0:1, :]
        for k in range(1, 8):
            listed = jnp.logical_or(listed, jid == clane[k : k + 1, :])

        def squares(i, carry):
            v = tabf[:, pl.ds(pl.multiple_of(i * LINE, LINE), LINE)].astype(F32)
            w3[pl.ds(pl.multiple_of(i * BINS, BINS), BINS), :] = v * v
            return carry

        lax.fori_loop(0, lines, squares, 0)
        bpscr[...] = jnp.zeros(bpscr.shape, F32)
        gscr[...] = jnp.zeros(gscr.shape, F32)

        for q in range(COLOURS):
            for e in range(8, 16):
                ag_in(q, e).wait_recv()
            p32 = pbuf[:, :, span(q)].astype(F32).reshape(NODES * ROWS, width)
            nz = noisev[:, span(q)]
            got = dot((p32 * nz).astype(BF16), rbuf[:, span(q)], NT)
            t32 = tabh[:, span(q)].astype(F32)
            ns = t32 * t32 * nz
            ns_hi = ns.astype(BF16)
            ns_lo = (ns - ns_hi.astype(F32)).astype(BF16)
            pp = p32 * p32
            pp_hi = pp.astype(BF16)
            pp_lo = (pp - pp_hi.astype(F32)).astype(BF16)
            power = dot(pp_hi, ns_hi, NT) + dot(pp_hi, ns_lo, NT) + dot(pp_lo, ns_hi, NT)
            bpscr[:, 0:BINS] += power
            for k in range(5):
                w = min(128, 576 - 128 * k)
                gscr[k, :, 0:w] += got[:, 128 * k : 128 * k + w]
        even, odd = pl.ds(0, 64, stride=2), pl.ds(1, 64, stride=2)
        ge = [gscr[k, even, :] for k in range(5)]
        go = [gscr[k, odd, :] for k in range(5)]
        sx[core, 0] = ge[0] + go[2]
        sx[core, 1] = go[1] - ge[3]
        sx[core, 2] = ge[4] + pltpu.roll(go[4], 96, 1)
        sx[core, 3] = bpscr[even, :] + bpscr[odd, :]
        trade = pltpu.make_async_remote_copy(
            src_ref=sx.at[core], dst_ref=sx.at[core], send_sem=sx_sem.at[0], recv_sem=sx_sem.at[1],
            device_id=mate, device_id_type=MESH,
        )
        trade.start()
        trade.wait_recv()

        quad = 0.5 * dot(sx[0, 3] + sx[1, 3], ohb, NN, HIGH)
        base = sx[0, 0] + sx[1, 0] - quad
        turn = sx[0, 1] + sx[1, 1]
        first = jnp.logical_and(listed, lanes < 32)
        s_plus = jnp.where(listed, base - turn, NEG)
        s_minus = jnp.where(listed, base + turn, NEG)
        s_zero = jnp.where(first, sx[0, 2] + sx[1, 2] - quad, NEG)
        peak = jnp.max(jnp.maximum(jnp.maximum(s_plus, s_minus), s_zero), axis=0, keepdims=True)
        peak = jnp.maximum(peak, pltpu.roll(peak, 32, 1))
        peak = jnp.maximum(peak, pltpu.roll(peak, 64, 1))
        e_plus = jnp.where(listed, jnp.exp(s_plus - peak), 0.0)
        e_minus = jnp.where(listed, jnp.exp(s_minus - peak), 0.0)
        e_zero = jnp.where(first, jnp.exp(s_zero - peak), 0.0)
        total = jnp.sum(e_plus + e_minus + e_zero, axis=0, keepdims=True)
        total = total + pltpu.roll(total, 32, 1)
        total = total + pltpu.roll(total, 64, 1)
        inv = 1.0 / total
        both = (e_plus + e_minus) * inv
        gap = (e_plus - e_minus) * inv
        zero = e_zero * inv
        blank = jnp.zeros((64, 128), F32)
        for k, (a, b) in enumerate(
            ((both, blank), (blank, -gap), (blank, both), (gap, blank), (zero, pltpu.roll(zero, 32, 1)))
        ):
            cscr[k, even, :] = a
            cscr[k, odd, :] = b
        share = dot(both + zero, ohb, NT, HIGH)
        bsscr[even, :] = share
        bsscr[odd, :] = blank
        coef = jnp.concatenate([cscr[k] for k in range(5)], axis=1)[:, 0:576].astype(BF16)
        dbuf[:, :, half : half + 128] = bsscr[...].reshape(NODES, ROWS, 128).astype(BF16)

        def rspan(q):
            return slice(q * width, (q + 1) * width + (128 if q == COLOURS - 1 else 0))

        def rs(q, e):
            m = at(offset_of(q, e))
            return pltpu.make_async_remote_copy(
                src_ref=dbuf.at[m, :, rspan(q)], dst_ref=rsb.at[e, :, rspan(q)],
                send_sem=rs_s.at[q, e], recv_sem=rs_r.at[q, e],
                device_id=dev(STEPS[(top(e) + q) % 4]), device_id_type=MESH,
            )

        def collect(q, e):
            m = at(offset_of(q, e))
            acc = dbuf[m, :, rspan(q)].astype(F32)
            for r in range(3, top(e) if e else -1, -1):
                child = e | 1 << r
                rs(q, child).wait_recv()
                acc = acc + rsb[child, :, rspan(q)].astype(F32)
            return m, acc

        for q in range(COLOURS):
            out = dot(coef, rbuf[:, span(q)])
            dbuf[:, :, span(q)] = out.reshape(NODES, ROWS, width).astype(BF16)
            for e in range(15, 7, -1):
                push(rs(q, e))
        for e in range(7, 0, -1):
            for q in range(COLOURS):
                m, acc = collect(q, e)
                dbuf[m, :, rspan(q)] = acc.astype(BF16)
                push(rs(q, e))
        extra = None
        for q in range(COLOURS):
            _, acc = collect(q, 0)
            zb[core, :, span(q)] = acc[:, :width].astype(BF16)
            if q == COLOURS - 1:
                extra = acc[:, width:]
        zx = pltpu.make_async_remote_copy(
            src_ref=zb.at[core], dst_ref=zb.at[core], send_sem=zx_sem.at[0], recv_sem=zx_sem.at[1],
            device_id=mate, device_id_type=MESH,
        )
        zx.start()

        rows8 = lax.broadcasted_iota(jnp.int32, (8, 128), 0)
        for j in range(2):
            wzs[j : j + 1, :] = jnp.sum(
                jnp.where(rows8 == 4 * core + 2 * j, extra, 0.0), axis=0, keepdims=True
            )
        order = sorted(range(1, groups), key=lambda k: -min(k, groups - k))

        def wmsg(k):
            return pltpu.make_async_remote_copy(
                src_ref=wzs, dst_ref=wzr.at[k], send_sem=w_s.at[k], recv_sem=w_r.at[k],
                device_id=((z + k) % groups, d), device_id_type=MESH,
            )

        def zmsg(k):
            return pltpu.make_async_remote_copy(
                src_ref=zsend.at[(z + k) % groups, 0 : 4 * CAP], dst_ref=zrecv.at[k, 0 : 4 * CAP],
                send_sem=z_s.at[k], recv_sem=z_r.at[k],
                device_id=((z + k) % groups, d), device_id_type=MESH,
            )

        for k in order:
            push(wmsg(k))
        zx.wait_recv()
        stack = jnp.concatenate(
            [
                zb[h, :, LINE * i : LINE * i + LINE].astype(F32)
                for h in range(2)
                for i in range(hl)
            ],
            axis=0,
        ).astype(BF16)
        packed = dot(sel[...], stack)
        zsend[...] = packed.astype(BF16).reshape(groups, slots, LINE)
        for k in order:
            push(zmsg(k))
        acc_w = wzs[...]
        for k in range(1, groups):
            wmsg(k).wait_recv()
            acc_w = acc_w + wzr[k]
        spread = (
            lax.broadcasted_iota(jnp.int32, (128, lines * BINS), 1) % BINS
            == lax.broadcasted_iota(jnp.int32, (128, lines * BINS), 0)
        ).astype(F32)
        scale = 64.0 / (16 * groups * NODES * 2)
        tall = jnp.concatenate(
            [jnp.broadcast_to(acc_w[j : j + 1, :] * scale, (8, 128)) for j in range(2)], axis=0
        )
        coefw = dot(tall, spread, NN, HIGH)
        slot = lax.broadcasted_iota(jnp.int32, (16, lines * BINS), 0) % 8
        ok = wkey[...].astype(jnp.int32) == z * 8 + slot
        weights = dot(jnp.where(ok, coefw, 0.0), w3[...], NN, HIGH)
        for j in range(2):
            o_weight[j] = weights[8 * j : 8 * j + CAP, :]
        acc = zsend[z, 0 : 4 * CAP].astype(F32)
        for k in range(1, groups):
            zmsg(k).wait_recv()
            acc = acc + zrecv[k, 0 : 4 * CAP].astype(F32)
        for r in range(4):
            o_data[r] = acc[CAP * r : CAP * r + CAP, :]

        for c in sent:
            c.wait_send()
        for c in swaps:
            c.wait_send()
        trade.wait_send()
        zx.wait_send()

    return kernel


def body(particles, defocus_bin, candidates, projections, ctf_table, inv_noise, line_slab, slab_owner):
    groups = lax.axis_size("grp")
    pixels = particles.shape[2]
    lines = pixels // LINE
    half = pixels // 2
    trig = jnp.asarray(phase_rows(lines))
    hbm = pl.BlockSpec(memory_space=pl.ANY)
    vmem = pl.BlockSpec(memory_space=pltpu.VMEM)
    smem = pl.BlockSpec(memory_space=pltpu.SMEM)
    dma = pltpu.SemaphoreType.DMA
    data, weight = pl.pallas_call(
        make_kernel(lines, groups),
        name="estep",
        out_shape=(
            jax.ShapeDtypeStruct((4, CAP, LINE), F32),
            jax.ShapeDtypeStruct((2, CAP, LINE), F32),
        ),
        in_specs=[hbm, hbm, hbm, hbm, hbm, vmem, vmem, vmem, smem],
        out_specs=(vmem, vmem),
        scratch_shapes=[
            pltpu.VMEM((2, 2, 16, half), BF16),
            pltpu.VMEM((2, 2, 2, half), BF16),
            pltpu.VMEM((2, 16, 8), jnp.int32),
            pltpu.VMEM((2, 1, 16), jnp.int32),
            pltpu.VMEM((8, half), F32),
            pltpu.VMEM((BINS, half), BF16),
            pltpu.VMEM((BINS, pixels), BF16),
            pltpu.VMEM((1, half), F32),
            pltpu.VMEM((8, half), F32),
            pltpu.VMEM((NODES, ROWS, half), BF16),
            pltpu.VMEM((576, half), BF16),
            pltpu.VMEM((5, 128, 128), F32),
            pltpu.VMEM((128, 128), F32),
            pltpu.VMEM((2, 4, 64, 128), F32),
            pltpu.VMEM((5, 128, 128), F32),
            pltpu.VMEM((128, 128), F32),
            pltpu.VMEM((NODES, ROWS, half + 128), BF16),
            pltpu.VMEM((NODES, ROWS, half + 128), BF16),
            pltpu.VMEM((2, ROWS, half), BF16),
            pltpu.VMEM((groups * 32, lines * ROWS), BF16),
            pltpu.VMEM((16, lines * BINS), F32),
            pltpu.VMEM((lines * BINS, LINE), F32),
            pltpu.VMEM((groups, 32, LINE), BF16),
            pltpu.VMEM((groups, 32, LINE), BF16),
            pltpu.VMEM((2, 128), F32),
            pltpu.VMEM((groups, 2, 128), F32),
            dma((8,)), dma((4,)), dma((4,)),
            dma((4, 16)), dma((4, 16)), dma((4, 16)), dma((4, 16)),
            dma((2,)), dma((2,)),
            dma((groups,)), dma((groups,)), dma((groups,)), dma((groups,)),
        ],
        compiler_params=pltpu.CompilerParams(
            collective_id=0, has_side_effects=True, vmem_limit_bytes=48 << 20
        ),
    )(
        jnp.transpose(particles, (1, 0, 2)),
        projections,
        ctf_table,
        inv_noise.reshape(1, pixels),
        trig,
        candidates,
        defocus_bin.reshape(1, 16),
        line_slab,
        slab_owner,
    )
    return (data.reshape(1, 2, 2, CAP, LINE), weight[None])


def solution(mesh):
    return jax.shard_map(
        body,
        mesh=mesh,
        in_specs=(
            P(("grp", "dev"), None, None),
            P(("grp", "dev")),
            P(("grp", "dev"), None),
            P("dev", None, None),
            P(),
            P(),
            P("dev", None),
            P(),
        ),
        out_specs=(P("grp", "dev", None, None, None), P("grp", "dev", None, None)),
        check_vma=False,
    )
```

time: 497 us -> 62.9 us (0.13)
  the two profiles are of different devices: /device:TPU:4 before, /device:TPU:1 now
where the time goes in v1:
time: 62.9 us; the launch traced here: 62.7 us
  Pallas kernels  58.2 us (93%)
  local copies, waits for them, and re-layouts  3.77 us (6%)
  between operations  0.71 us (1%)
    pallas_call x1, Pallas kernels, body(): pl.pallas_call(make_kernel(lines, groups), name='estep', out_shape=(jax.S...  58.2 us
    unnamed x18, local copies, waits for them, and re-layouts  3.77 us

profile of v1, /device:TPU:1, one launch (start us, length us, event | category | flops | bytes accessed | tf_op | source)
XLA Modules:
  0.0 62.7 jit_solution(3480849180915518491)
XLA Ops:
  0.6 0.8 %copy.12.cand = s32[16,8]{1,0:T(8,128)S(1)} copy(s32[16,8]{0,1:T(8,128)} %param.11) | data formatting | bytes 1024 | tf_op args[2]
  1.4 0.0 copy-start
  1.4 0.0 copy-start.1
  1.4 0.0 copy-start.2
  1.4 0.0 copy-start.3
  1.4 0.0 copy-start.6
  1.4 1.2 %copy.16 = bf16[16,2,6144]{2,0,1:T(8,128)(2,1)S(1)} copy(bf16[16,2,6144]{2,1,0:T(2,128)(2,1)} %param.9) | data formatting | bytes 786432 | tf_op args[0]
  2.6 0.0 copy-start.4
  2.6 0.0 copy-start.5
  2.6 0.0 copy-done
  2.6 0.0 copy-done.1
  2.6 0.0 copy-done.2
  2.6 0.0 copy-done.3
  2.6 0.0 copy-done.6
  2.7 0.6 copy-done.4
  3.3 0.0 copy-done.5
  3.3 58.2 %estep.1 = (f32[4,6,128]{2,1,0:T(8,128)S(1)}, f32[2,6,128]{2,1,0:T(8,128)S(1)}) custom-call(bf16[2,16,6144]{2,1,0:T(8,128)(2,1)S(1)} %bitcast.7, bf16[2,2,6144]{2,1,0:T(2,128)(2,1)S(1)} %copy-done.2, bf16[16,6144]{1,0:T(8,128)(2,1)S(1)} %copy-done, f32[1,6144]{1,0:T(1,128)S(1)} %bitcast.8, f32[8,6144]{1,0:T(8,128)S(1)} %copy-done.1, s32[16,8]{1,0:T(8,128)S(1)} %copy.12.cand, ...), custom_call_target="tpu_custom_call" | custom-call | tf_op jit(solution)/shard_map/estep/pallas_call | solution.py:463
  61.5 0.6 copy.13
  62.1 0.6 copy.14
Async XLA Ops:
  1.4 1.2 %copy-start = (bf16[16,6144]{1,0:T(8,128)(2,1)S(1)}, bf16[16,6144]{1,0:T(8,128)(2,1)}, u32[]{:S(2)}) copy-start(bf16[16,6144]{1,0:T(8,128)(2,1)} %table.1) | copy-start | bytes 589828
  1.4 1.2 %copy-start.1 = (f32[8,6144]{1,0:T(8,128)S(1)}, f32[8,6144]{1,0:T(8,128)}, u32[]{:S(2)}) copy-start(f32[8,6144]{1,0:T(8,128)} %constant.2.clone.trig) | copy-start | bytes 589828
  1.4 1.2 %copy-start.2 = (bf16[2,2,6144]{2,1,0:T(2,128)(2,1)S(1)}, bf16[2,2,6144]{2,1,0:T(2,128)(2,1)}, u32[]{:S(2)}) copy-start(bf16[2,2,6144]{2,1,0:T(2,128)(2,1)} %proj.1) | copy-start | bytes 147460
  1.4 1.2 %copy-start.3 = (f32[6144]{0:T(1024)S(1)}, f32[6144]{0:T(1024)}, u32[]{:S(2)}) copy-start(f32[6144]{0:T(1024)} %param.14) | copy-start | bytes 73732
  1.4 1.2 %copy-start.6 = (s32[16]{0:T(128)S(1)}, s32[16]{0:T(128)}, u32[]{:S(2)}) copy-start(s32[16]{0:T(128)} %owner.1) | copy-start | bytes 196
  2.6 0.7 %copy-start.4 = (s32[2,48]{1,0:T(2,128)S(1)}, s32[2,48]{1,0:T(2,128)}, u32[]{:S(2)}) copy-start(s32[2,48]{1,0:T(2,128)} %slab.1) | copy-start | bytes 1156
  2.6 0.7 %copy-start.5 = (s32[16]{0:T(128)S(1)}, s32[16]{0:T(128)}, u32[]{:S(2)}) copy-start(s32[16]{0:T(128)} %param.10) | copy-start | bytes 196

commit v2 on v1

v2 whole, which is shorter than its diff:
```python
import math

import jax
import jax.numpy as jnp
import numpy as np
from jax import lax
from jax.experimental import pallas as pl
from jax.experimental.pallas import tpu as pltpu
from jax.sharding import PartitionSpec as P

LINE = 128
CAP = 6
BINS = 16
NODES = 16
COLOURS = 4
ROWS = 8
NEG = -3.0e38
MESH = pl.DeviceIdType.MESH
F32 = jnp.float32
BF16 = jnp.bfloat16
HIGH = lax.Precision.HIGHEST
NN = (((1,), (0,)), ((), ()))
NT = (((1,), (1,)), ((), ()))
TN = (((0,), (0,)), ((), ()))
STAGES = (
    ((1, 4, 5), (3, 12, 15)),
    ((3, 12, 15), (1, 4, 5)),
    ((1, 12, 13), (3, 4, 7)),
    ((3, 4, 7), (1, 12, 13)),
)
NEAR = (1, 3, 4, 12, 5, 15, 13, 7)


def dot(a, b, dims=NN, precision=None):
    return lax.dot_general(a, b, dims, preferred_element_type=F32, precision=precision)


def phase_rows(lines):
    line = np.repeat(np.arange(lines), LINE).astype(np.float64)
    column = np.tile(np.arange(LINE), lines)
    freq = np.where(column < LINE // 2, column, column - LINE).astype(np.float64)
    moves = ((0, 1), (1, -1), (1, 0), (1, 1))
    angle = np.stack([dx * line + dy * freq for dx, dy in moves]) * (2.0 * math.pi / LINE)
    return np.concatenate([np.cos(angle), np.sin(angle)]).astype(np.float32)


def flip(v, k):
    if k == 0:
        return v
    if k == 1:
        return v + 1 - 2 * (v % 2)
    if k == 2:
        return (v + 2) % 4
    return 3 - v


def make_kernel(lines, groups):
    half = lines * LINE // 2
    width = half // COLOURS
    hl = lines // 2
    slots = 32

    def kernel(parts, proj, table, noise, trig, cand, bins, slab, owner,
               o_data, o_weight,
               xin, xs, ctfv, candb, binb, slabv, owners, trigv, tabh, tabf, noisev, pbuf, ps, rbuf,
               gscr, bpscr, sx, cscr, bsscr, dbuf, rsb, zb, sel, wkey, w3, zsend, zrecv, wzs, wzr,
               loc, ex_s, ex_r, ag_s, ag_r, rs_s, rs_r, sx_sem, zx_sem, z_s, z_r, w_s, w_r, ring):
        z = lax.axis_index("grp")
        d = lax.axis_index("dev")
        core = d % 2
        node = d // 2
        nx, ny = node % 4, node // 4
        other = 1 - core

        def dev(k, c):
            return (z, (flip(ny, k // 4) * 4 + flip(nx, k % 4)) * 2 + c)

        def along(k):
            return ((z + k + groups) % groups, d)

        mate = (z, node * 2 + other)

        def greet(sem, to):
            pl.semaphore_signal(sem, inc=1, device_id=to, device_id_type=MESH)

        barrier = pltpu.get_barrier_semaphore()
        greet(barrier, mate)
        for k in NEAR:
            greet(barrier, dev(k, core))
            greet(barrier, dev(k, other))
        greet(barrier, along(1))
        greet(barrier, along(-1))

        mine = pl.multiple_of(core * half, LINE)
        theirs = pl.multiple_of(other * half, LINE)
        loads = [
            pltpu.make_async_copy(bins, binb.at[core], loc.at[0]),
            pltpu.make_async_copy(table.at[:, pl.ds(mine, half)], tabh, loc.at[1]),
            pltpu.make_async_copy(parts.at[:, :, pl.ds(mine, half)], xin.at[core], loc.at[2]),
            pltpu.make_async_copy(trig.at[:, pl.ds(mine, half)], trigv, loc.at[3]),
            pltpu.make_async_copy(proj.at[:, :, pl.ds(mine, half)], pbuf.at[0, core], loc.at[4]),
            pltpu.make_async_copy(noise.at[:, pl.ds(mine, half)], noisev, loc.at[5]),
            pltpu.make_async_copy(cand, candb.at[core], loc.at[6]),
            pltpu.make_async_copy(slab, slabv, loc.at[7]),
            pltpu.make_async_copy(table, tabf, loc.at[8]),
            pltpu.make_async_copy(owner, owners, loc.at[9]),
        ]
        for c in loads:
            c.start()

        pl.semaphore_wait(barrier, 3 + 2 * len(NEAR))

        def span(q):
            return slice(q * width, (q + 1) * width)

        def cast(q, t, c):
            side = pl.multiple_of((mine if c is core else theirs) + q * width, LINE)
            return pltpu.make_async_remote_copy(
                src_ref=proj.at[:, :, pl.ds(side, width)],
                dst_ref=pbuf.at[t, core, :, :, span(q)],
                send_sem=ag_s.at[q, t, 0 if c is core else 1], recv_sem=ag_r.at[q, t, core],
                device_id=dev(t, c), device_id_type=MESH,
            )

        def relay(q, k, s, t):
            return pltpu.make_async_remote_copy(
                src_ref=pbuf.at[k, s, :, :, span(q)], dst_ref=pbuf.at[k ^ t, s, :, :, span(q)],
                send_sem=ag_s.at[q, k ^ t, s], recv_sem=ag_r.at[q, k ^ t, s],
                device_id=dev(t, core), device_id_type=MESH,
            )

        def arrived(q, k, s):
            pltpu.make_async_remote_copy(
                src_ref=pbuf.at[k, s, :, :, span(q)], dst_ref=pbuf.at[k, s, :, :, span(q)],
                send_sem=ag_s.at[q, k, s], recv_sem=ag_r.at[q, k, s],
                device_id=dev(k, core), device_id_type=MESH,
            ).wait_recv()

        sent = []

        def push(c):
            c.start()
            sent.append(c)

        for stage in range(2):
            for i in (2, 0, 1):
                for q in range(COLOURS):
                    push(cast(q, STAGES[q][stage][i], core))
                    push(cast(q, STAGES[q][stage][i], other))
        swaps = [
            pltpu.make_async_remote_copy(
                src_ref=src, dst_ref=dst, send_sem=ex_s.at[i], recv_sem=ex_r.at[i],
                device_id=mate, device_id_type=MESH,
            )
            for i, (src, dst) in enumerate(
                (
                    (proj.at[:, :, pl.ds(theirs, half)], pbuf.at[0, core]),
                    (bins, binb.at[core]),
                    (cand, candb.at[core]),
                    (parts.at[:, :, pl.ds(theirs, half)], xin.at[core]),
                )
            )
        ]
        for c in swaps:
            push(c)
        reach = 1
        rounds = []
        while 2 * reach <= groups // 2:
            rounds.append(reach)
            reach *= 2
        if rounds:
            greet(ring.at[0], along(1))
            greet(ring.at[0], along(-1))

        def spread_word(i):
            if i < len(rounds):
                pl.semaphore_wait(ring.at[i], 2)
                if i + 1 < len(rounds):
                    greet(ring.at[i + 1], along(rounds[i + 1]))
                    greet(ring.at[i + 1], along(-rounds[i + 1]))

        even2, odd2 = pl.ds(0, 16, stride=2), pl.ds(1, 16, stride=2)
        bid = lax.broadcasted_iota(jnp.int32, (BINS, 16), 0)

        def rotate(s):
            hot = (bid == binb[s]).astype(F32).astype(BF16)
            ctfv[...] = dot(hot, tabh[...], TN)

            def chunk(i, carry):
                for t in range(width // LINE):
                    at_ = pl.ds(pl.multiple_of(i * width + t * LINE, LINE), LINE)
                    for p in range(16):
                        xs[t, 2 * p : 2 * p + 2, :] = xin[s, p, :, at_].astype(F32)
                    for part in range(2):
                        x = ctfv[:, at_] * xs[t, even2 if part == 0 else odd2, :]
                        r0 = pl.multiple_of(512 + part * 32 + s * 16, 16)
                        rbuf[pl.ds(r0, 16), at_] = x.astype(BF16)
                        for u in range(8):
                            r0 = pl.multiple_of(part * 256 + u * 32 + s * 16, 16)
                            rbuf[pl.ds(r0, 16), at_] = (x * trigv[u : u + 1, at_]).astype(BF16)
                return carry

            lax.fori_loop(0, COLOURS, chunk, 0)

        for i in range(4):
            loads[i].wait()
        rotate(core)
        for i in range(3):
            for q in range(COLOURS):
                k = STAGES[q][0][i]
                for s in range(2):
                    arrived(q, k, s)
                    for t in STAGES[q][1][::-1]:
                        push(relay(q, k, s, t))
        spread_word(0)
        swaps[1].wait_recv()
        swaps[3].wait_recv()
        rotate(other)

        for i in range(4, 10):
            loads[i].wait()
        swaps[2].wait_recv()
        lanes = lax.broadcasted_iota(jnp.int32, (1, 128), 1)
        cid = lax.broadcasted_iota(jnp.int32, (128, 128), 0)
        lane_core = (lanes % 32) // 16
        til = (
            lax.broadcasted_iota(jnp.int32, (16, 128), 1) % 16
            == lax.broadcasted_iota(jnp.int32, (16, 128), 0)
        ).astype(F32)
        bl = [dot(binb[s].astype(F32), til) for s in range(2)]
        blane = jnp.where(lane_core == 1, bl[1], bl[0]).astype(jnp.int32)
        ohb = (cid == blane).astype(F32)
        cl = [dot(candb[s].astype(F32), til) for s in range(2)]
        clane = jnp.where(lane_core == 1, cl[1], cl[0]).astype(jnp.int32)
        rid = lax.broadcasted_iota(jnp.int32, (64, 128), 0)
        jid = ((rid // 4) ^ node) * 4 + rid % 4
        listed = jid == clane[0:1, :]
        for k in range(1, 8):
            listed = jnp.logical_or(listed, jid == clane[k : k + 1, :])
        bpscr[...] = jnp.zeros(bpscr.shape, F32)
        gscr[...] = jnp.zeros(gscr.shape, F32)
        spread_word(1)

        def score(q, ks):
            for i, k in enumerate(ks):
                for s in range(2):
                    for j in range(2):
                        r = 8 * i + 4 * s + 2 * j
                        ps[r : r + 2, :] = pbuf[k, s, j, :, span(q)].astype(F32)
            p32 = ps[0 : 8 * len(ks), :]
            nz = noisev[:, span(q)]
            got = dot((p32 * nz).astype(BF16), rbuf[:, span(q)], NT)
            t32 = tabh[:, span(q)].astype(F32)
            ns = t32 * t32 * nz
            ns_hi = ns.astype(BF16)
            ns_lo = (ns - ns_hi.astype(F32)).astype(BF16)
            pp = p32 * p32
            pp_hi = pp.astype(BF16)
            pp_lo = (pp - pp_hi.astype(F32)).astype(BF16)
            power = dot(pp_hi, ns_hi, NT) + dot(pp_hi, ns_lo, NT) + dot(pp_lo, ns_hi, NT)
            for i, k in enumerate(ks):
                here, there = slice(8 * i, 8 * i + 8), slice(8 * k, 8 * k + 8)
                bpscr[there, 0:BINS] += power[here, :]
                for b in range(5):
                    w = min(128, 576 - 128 * b)
                    gscr[b, there, 0:w] += got[here, 128 * b : 128 * b + w]

        swaps[0].wait_recv()
        for q in range(COLOURS):
            for k in STAGES[q][1]:
                for s in range(2):
                    arrived(q, k, s)
            score(q, (0,) + STAGES[q][0] + STAGES[q][1])
        for q in range(COLOURS):
            late = tuple(a ^ b for a in STAGES[q][0] for b in STAGES[q][1])
            for k in late:
                for s in range(2):
                    arrived(q, k, s)
            score(q, late)
        even, odd = pl.ds(0, 64, stride=2), pl.ds(1, 64, stride=2)
        ge = [gscr[k, even, :] for k in range(5)]
        go = [gscr[k, odd, :] for k in range(5)]
        sx[core, 0] = ge[0] + go[2]
        sx[core, 1] = go[1] - ge[3]
        sx[core, 2] = jnp.where(
            lanes < 32, ge[4] + pltpu.roll(go[4], 96, 1), pltpu.roll(bpscr[even, :] + bpscr[odd, :], 64, 1)
        )
        trade = pltpu.make_async_remote_copy(
            src_ref=sx.at[core], dst_ref=sx.at[core], send_sem=sx_sem.at[0], recv_sem=sx_sem.at[1],
            device_id=mate, device_id_type=MESH,
        )
        push(trade)
        trade.wait_recv()

        last = sx[0, 2] + sx[1, 2]
        power = jnp.where(lanes < BINS, pltpu.roll(last, 64, 1), 0.0)
        quad = 0.5 * dot(power, ohb, NN, HIGH)
        base = sx[0, 0] + sx[1, 0] - quad
        turn = sx[0, 1] + sx[1, 1]
        first = jnp.logical_and(listed, lanes < 32)
        s_plus = jnp.where(listed, base - turn, NEG)
        s_minus = jnp.where(listed, base + turn, NEG)
        s_zero = jnp.where(first, last - quad, NEG)
        peak = jnp.max(jnp.maximum(jnp.maximum(s_plus, s_minus), s_zero), axis=0, keepdims=True)
        peak = jnp.maximum(peak, pltpu.roll(peak, 32, 1))
        peak = jnp.maximum(peak, pltpu.roll(peak, 64, 1))
        e_plus = jnp.where(listed, jnp.exp(s_plus - peak), 0.0)
        e_minus = jnp.where(listed, jnp.exp(s_minus - peak), 0.0)
        e_zero = jnp.where(first, jnp.exp(s_zero - peak), 0.0)
        total = jnp.sum(e_plus + e_minus + e_zero, axis=0, keepdims=True)
        total = total + pltpu.roll(total, 32, 1)
        total = total + pltpu.roll(total, 64, 1)
        inv = 1.0 / total
        both = (e_plus + e_minus) * inv
        gap = (e_plus - e_minus) * inv
        zero = e_zero * inv
        blank = jnp.zeros((64, 128), F32)
        for k, (a, b) in enumerate(
            ((both, blank), (blank, -gap), (blank, both), (gap, blank), (zero, pltpu.roll(zero, 32, 1)))
        ):
            cscr[k, even, :] = a
            cscr[k, odd, :] = b
        share = dot(both + zero, ohb, NT, HIGH)
        bsscr[even, :] = share
        bsscr[odd, :] = blank
        coef = jnp.concatenate([cscr[k] for k in range(5)], axis=1)[:, 0:576].astype(BF16)
        dbuf[:, :, half : half + 128] = bsscr[...].reshape(NODES, ROWS, 128).astype(BF16)

        def rspan(q):
            return slice(q * width, (q + 1) * width + (128 if q == COLOURS - 1 else 0))

        def rs(q, k, t):
            return pltpu.make_async_remote_copy(
                src_ref=dbuf.at[k, :, rspan(q)], dst_ref=rsb.at[k, :, rspan(q)],
                send_sem=rs_s.at[q, k], recv_sem=rs_r.at[q, k],
                device_id=dev(t, core), device_id_type=MESH,
            )

        def collect(q, k, froms):
            acc = dbuf[k, :, rspan(q)].astype(F32)
            for child in froms:
                rs(q, child, child ^ k).wait_recv()
                acc = acc + rsb[child, :, rspan(q)].astype(F32)
            return acc

        for q in range(COLOURS):
            out = dot(coef, rbuf[:, span(q)])
            dbuf[:, :, span(q)] = out.reshape(NODES, ROWS, width).astype(BF16)
            for k in STAGES[q][0] + (0,):
                for t in STAGES[q][1][::-1]:
                    push(rs(q, k ^ t, t))

        lid = lax.broadcasted_iota(jnp.int32, (groups, lines), 0)
        tri = (
            lax.broadcasted_iota(jnp.int32, (lines, lines), 0)
            < lax.broadcasted_iota(jnp.int32, (lines, lines), 1)
        ).astype(F32)
        wide = (
            lax.broadcasted_iota(jnp.int32, (lines, lines * ROWS), 1) // ROWS
            == lax.broadcasted_iota(jnp.int32, (lines, lines * ROWS), 0)
        ).astype(F32)
        wide16 = (
            lax.broadcasted_iota(jnp.int32, (lines, lines * BINS), 1) // BINS
            == lax.broadcasted_iota(jnp.int32, (lines, lines * BINS), 0)
        ).astype(F32)
        keys = []
        for j in range(2):
            row = slabv[j : j + 1, :]
            own = jnp.zeros((1, lines), jnp.int32)
            for s in range(groups):
                own = own + jnp.where(row == s, owners[0, s], 0)
            hit = (lid == own).astype(F32)
            rank = jnp.sum(hit * dot(hit, tri), axis=0, keepdims=True)
            keys.append((own * 8).astype(F32) + rank)
        key8 = [dot(k, wide) for k in keys]
        col = lax.broadcasted_iota(jnp.int32, (1, lines * ROWS), 1) % ROWS
        pick = jnp.where(col % 4 >= 2, key8[1], key8[0]).astype(jnp.int32) * 8 + col
        rid = lax.broadcasted_iota(jnp.int32, (groups * slots, lines * ROWS), 0)
        inner = rid % slots
        r4 = (
            (inner >= CAP).astype(jnp.int32)
            + (inner >= 2 * CAP).astype(jnp.int32)
            + (inner >= 3 * CAP).astype(jnp.int32)
            + (inner >= 4 * CAP).astype(jnp.int32)
        )
        want = ((rid // slots) * 8 + (inner - CAP * r4)) * 8 + 4 * core + r4
        sel[...] = (want == pick).astype(F32).astype(BF16)
        for j in range(2):
            wkey[8 * j : 8 * j + 8, :] = jnp.broadcast_to(dot(keys[j], wide16), (8, lines * BINS))

        for i in range(3):
            for q in range(COLOURS):
                k = STAGES[q][0][i]
                acc = collect(q, k, [k ^ t for t in STAGES[q][1]])
                dbuf[k, :, rspan(q)] = acc.astype(BF16)
                push(rs(q, k, k))

        def squares(i, carry):
            v = tabf[:, pl.ds(pl.multiple_of(i * LINE, LINE), LINE)].astype(F32)
            w3[pl.ds(pl.multiple_of(i * BINS, BINS), BINS), :] = v * v
            return carry

        lax.fori_loop(0, lines, squares, 0)
        spread_word(2)
        extra = None
        for q in range(COLOURS):
            acc = collect(q, 0, STAGES[q][1] + STAGES[q][0])
            zb[core, :, span(q)] = acc[:, :width].astype(BF16)
            if q == COLOURS - 1:
                extra = acc[:, width:]
        zx = pltpu.make_async_remote_copy(
            src_ref=zb.at[core], dst_ref=zb.at[core], send_sem=zx_sem.at[0], recv_sem=zx_sem.at[1],
            device_id=mate, device_id_type=MESH,
        )
        push(zx)

        rows8 = lax.broadcasted_iota(jnp.int32, (8, 128), 0)
        for j in range(2):
            wzs[j : j + 1, :] = jnp.sum(
                jnp.where(rows8 == 4 * core + 2 * j, extra, 0.0), axis=0, keepdims=True
            )
        order = sorted(range(1, groups), key=lambda k: -min(k, groups - k))

        def wmsg(k):
            return pltpu.make_async_remote_copy(
                src_ref=wzs, dst_ref=wzr.at[k], send_sem=w_s.at[k], recv_sem=w_r.at[k],
                device_id=((z + k) % groups, d), device_id_type=MESH,
            )

        def zmsg(k):
            return pltpu.make_async_remote_copy(
                src_ref=zsend.at[(z + k) % groups, 0 : 4 * CAP], dst_ref=zrecv.at[k, 0 : 4 * CAP],
                send_sem=z_s.at[k], recv_sem=z_r.at[k],
                device_id=((z + k) % groups, d), device_id_type=MESH,
            )

        for k in order:
            push(wmsg(k))
        zx.wait_recv()
        stack = jnp.concatenate(
            [
                zb[h, :, LINE * i : LINE * i + LINE].astype(F32)
                for h in range(2)
                for i in range(hl)
            ],
            axis=0,
        ).astype(BF16)
        packed = dot(sel[...], stack)
        zsend[...] = packed.astype(BF16).reshape(groups, slots, LINE)
        for k in order:
            push(zmsg(k))
        acc_w = wzs[...]
        for k in range(1, groups):
            wmsg(k).wait_recv()
            acc_w = acc_w + wzr[k]
        spread = (
            lax.broadcasted_iota(jnp.int32, (128, lines * BINS), 1) % BINS
            == lax.broadcasted_iota(jnp.int32, (128, lines * BINS), 0)
        ).astype(F32)
        scale = 64.0 / (16 * groups * NODES * 2)
        tall = jnp.concatenate(
            [jnp.broadcast_to(acc_w[j : j + 1, :] * scale, (8, 128)) for j in range(2)], axis=0
        )
        coefw = dot(tall, spread, NN, HIGH)
        slot = lax.broadcasted_iota(jnp.int32, (16, lines * BINS), 0) % 8
        ok = wkey[...].astype(jnp.int32) == z * 8 + slot
        weights = dot(jnp.where(ok, coefw, 0.0), w3[...], NN, HIGH)
        for j in range(2):
            o_weight[j] = weights[8 * j : 8 * j + CAP, :]
        acc = zsend[z, 0 : 4 * CAP].astype(F32)
        for k in range(1, groups):
            zmsg(k).wait_recv()
            acc = acc + zrecv[k, 0 : 4 * CAP].astype(F32)
        for r in range(4):
            o_data[r] = acc[CAP * r : CAP * r + CAP, :]

        for c in sent:
            c.wait_send()

    return kernel


def body(particles, defocus_bin, candidates, projections, ctf_table, inv_noise, line_slab, slab_owner):
    groups = lax.axis_size("grp")
    pixels = particles.shape[2]
    lines = pixels // LINE
    half = pixels // 2
    trig = jnp.asarray(phase_rows(lines))
    hbm = pl.BlockSpec(memory_space=pl.ANY)
    vmem = pl.BlockSpec(memory_space=pltpu.VMEM)
    dma = pltpu.SemaphoreType.DMA
    data, weight = pl.pallas_call(
        make_kernel(lines, groups),
        name="estep",
        out_shape=(
            jax.ShapeDtypeStruct((4, CAP, LINE), F32),
            jax.ShapeDtypeStruct((2, CAP, LINE), F32),
        ),
        in_specs=[hbm] * 9,
        out_specs=(vmem, vmem),
        scratch_shapes=[
            pltpu.VMEM((2, 16, 2, half), BF16),
            pltpu.VMEM((half // COLOURS // LINE, 32, LINE), F32),
            pltpu.VMEM((16, half), F32),
            pltpu.VMEM((2, 8, 16), jnp.int32),
            pltpu.VMEM((2, 1, 16), jnp.int32),
            pltpu.VMEM((2, lines), jnp.int32),
            pltpu.SMEM((1, groups), jnp.int32),
            pltpu.VMEM((8, half), F32),
            pltpu.VMEM((BINS, half), BF16),
            pltpu.VMEM((BINS, pixels), BF16),
            pltpu.VMEM((1, half), F32),
            pltpu.VMEM((NODES, 2, 2, 2, half), BF16),
            pltpu.VMEM((128, half // COLOURS), F32),
            pltpu.VMEM((576, half), BF16),
            pltpu.VMEM((5, 128, 128), F32),
            pltpu.VMEM((128, 128), F32),
            pltpu.VMEM((2, 3, 64, 128), F32),
            pltpu.VMEM((5, 128, 128), F32),
            pltpu.VMEM((128, 128), F32),
            pltpu.VMEM((NODES, ROWS, half + 128), BF16),
            pltpu.VMEM((NODES, ROWS, half + 128), BF16),
            pltpu.VMEM((2, ROWS, half), BF16),
            pltpu.VMEM((groups * 32, lines * ROWS), BF16),
            pltpu.VMEM((16, lines * BINS), F32),
            pltpu.VMEM((lines * BINS, LINE), F32),
            pltpu.VMEM((groups, 32, LINE), BF16),
            pltpu.VMEM((groups, 32, LINE), BF16),
            pltpu.VMEM((2, 128), F32),
            pltpu.VMEM((groups, 2, 128), F32),
            dma((10,)), dma((4,)), dma((4,)),
            dma((4, 16, 2)), dma((4, 16, 2)), dma((4, 16)), dma((4, 16)),
            dma((2,)), dma((2,)),
            dma((groups,)), dma((groups,)), dma((groups,)), dma((groups,)),
            pltpu.SemaphoreType.REGULAR((3,)),
        ],
        compiler_params=pltpu.CompilerParams(
            collective_id=0, has_side_effects=True, vmem_limit_bytes=67043328
        ),
    )(
        particles,
        projections,
        ctf_table,
        inv_noise.reshape(1, pixels),
        trig,
        candidates.T,
        defocus_bin.reshape(1, 16),
        line_slab,
        slab_owner.reshape(1, groups),
    )
    return (data.reshape(1, 2, 2, CAP, LINE), weight[None])


def solution(mesh):
    return jax.shard_map(
        body,
        mesh=mesh,
        in_specs=(
            P(("grp", "dev"), None, None),
            P(("grp", "dev")),
            P(("grp", "dev"), None),
            P("dev", None, None),
            P(),
            P(),
            P("dev", None),
            P(),
        ),
        out_specs=(P("grp", "dev", None, None, None), P("grp", "dev", None, None)),
        check_vma=False,
    )
```

time: 62.9 us -> 56.1 us (0.89)
  Pallas kernels: 58.2 us -> 53.4 us
  local copies, waits for them, and re-layouts: 3.77 us -> 1.93 us
    pallas_call x1, Pallas kernels: 58.2 us -> 53.4 us  [body(): pl.pallas_call(make_kernel(lines, groups), name='estep', out_shape=(jax.S...]
    unnamed x18 -> x4, local copies, waits for them, and re-layouts: 3.77 us -> 1.93 us
where the time goes in v2:
time: 56.1 us; the launch traced here: 56 us
  Pallas kernels  53.4 us (95%)
  local copies, waits for them, and re-layouts  1.93 us (3%)
  between operations  0.65 us (1%)
    pallas_call x1, Pallas kernels, body(): pl.pallas_call(make_kernel(lines, groups), name='estep', out_shape=(jax.S...  53.4 us
    unnamed x4, local copies, waits for them, and re-layouts  1.93 us

profile of v2, /device:TPU:1, one launch (start us, length us, event | category | flops | bytes accessed | tf_op | source)
XLA Modules:
  0.0 56.0 jit_solution(9867741113797599179)
XLA Ops:
  0.6 53.4 %estep.1 = (f32[4,6,128]{2,1,0:T(8,128)}, f32[2,6,128]{2,1,0:T(8,128)}) custom-call(bf16[16,2,6144]{2,1,0:T(2,128)(2,1)} %parts.1, bf16[2,2,6144]{2,1,0:T(2,128)(2,1)} %proj.1, bf16[16,6144]{1,0:T(8,128)(2,1)} %table.1, f32[1,6144]{1,0:T(1,128)} %bitcast.6, f32[8,6144]{1,0:T(8,128)} %constant.2.clone.trig, s32[8,16]{1,0:T(8,128)} %bitcast.9, ...), custom_call_target="tpu_custom_call" | custom-call | tf_op jit(solution)/shard_map/estep/pallas_call | solution.py:492
  54.0 0.0 copy-start
  54.0 1.3 %copy.11 = f32[1,2,2,6,128]{4,2,3,1,0:T(2,128)} copy(f32[1,2,2,6,128]{4,3,2,1,0:T(8,128)} %bitcast.7) | data formatting | bytes 24576
  55.4 0.0 copy-done
  55.4 0.6 %copy.12 = f32[1,2,6,128]{3,1,2,0:T(2,128)} copy(f32[1,2,6,128]{3,2,1,0:T(8,128)S(1)} %bitcast.8) | data formatting | bytes 12288
Async XLA Ops:
  54.0 1.3 %copy-start = (f32[2,6,128]{2,1,0:T(8,128)S(1)}, f32[2,6,128]{2,1,0:T(8,128)}, u32[]{:S(2)}) copy-start(f32[2,6,128]{2,1,0:T(8,128)} %get-tuple-element.5) | copy-start | bytes 18436

commit v3 on v2

--- a/solution.py
+++ b/solution.py
@@ -12,7 +12,8 @@
 CAP = 6
 BINS = 16
 NODES = 16
-COLOURS = 4
+COLOURS = 2
+CHUNKS = 4
 ROWS = 8
 NEG = -3.0e38
 MESH = pl.DeviceIdType.MESH
@@ -25,10 +26,8 @@
 STAGES = (
     ((1, 4, 5), (3, 12, 15)),
     ((3, 12, 15), (1, 4, 5)),
-    ((1, 12, 13), (3, 4, 7)),
-    ((3, 4, 7), (1, 12, 13)),
 )
-NEAR = (1, 3, 4, 12, 5, 15, 13, 7)
+NEAR = (1, 3, 4, 12, 5, 15)
 
 
 def dot(a, b, dims=NN, precision=None):
@@ -58,13 +57,14 @@
     half = lines * LINE // 2
     width = half // COLOURS
     hl = lines // 2
+    piece = half // CHUNKS
     slots = 32
 
     def kernel(parts, proj, table, noise, trig, cand, bins, slab, owner,
                o_data, o_weight,
-               xin, xs, ctfv, candb, binb, slabv, owners, trigv, tabh, tabf, noisev, pbuf, ps, rbuf,
+               xin, xs, ctfv, candb, binb, slabv, owners, trigv, tabh, tabf, noisev, nsv, pbuf, ps, rbuf,
                gscr, bpscr, sx, cscr, bsscr, dbuf, rsb, zb, sel, wkey, w3, zsend, zrecv, wzs, wzr,
-               loc, ex_s, ex_r, ag_s, ag_r, rs_s, rs_r, sx_sem, zx_sem, z_s, z_r, w_s, w_r, ring):
+               loc, ex_s, ex_r, ag_s, ag_a, ag_b, ag_l, rs_s, rs_a, rs_b, sx_sem, zx_sem, z_sem, w_sem, ring):
         z = lax.axis_index("grp")
         d = lax.axis_index("dev")
         core = d % 2
@@ -118,23 +118,22 @@
             return pltpu.make_async_remote_copy(
                 src_ref=proj.at[:, :, pl.ds(side, width)],
                 dst_ref=pbuf.at[t, core, :, :, span(q)],
-                send_sem=ag_s.at[q, t, 0 if c is core else 1], recv_sem=ag_r.at[q, t, core],
+                send_sem=ag_s.at[0],
+                recv_sem=ag_a.at[q, STAGES[q][0].index(t)] if t in STAGES[q][0] else ag_b.at[q],
                 device_id=dev(t, c), device_id_type=MESH,
             )
 
         def relay(q, k, s, t):
             return pltpu.make_async_remote_copy(
                 src_ref=pbuf.at[k, s, :, :, span(q)], dst_ref=pbuf.at[k ^ t, s, :, :, span(q)],
-                send_sem=ag_s.at[q, k ^ t, s], recv_sem=ag_r.at[q, k ^ t, s],
+                send_sem=ag_s.at[0], recv_sem=ag_l.at[q],
                 device_id=dev(t, core), device_id_type=MESH,
             )
 
-        def arrived(q, k, s):
-            pltpu.make_async_remote_copy(
-                src_ref=pbuf.at[k, s, :, :, span(q)], dst_ref=pbuf.at[k, s, :, :, span(q)],
-                send_sem=ag_s.at[q, k, s], recv_sem=ag_r.at[q, k, s],
-                device_id=dev(k, core), device_id_type=MESH,
-            ).wait_recv()
+        def settle(ref, send, recv):
+            return pltpu.make_async_remote_copy(
+                src_ref=ref, dst_ref=ref, send_sem=send, recv_sem=recv, device_id=mate, device_id_type=MESH,
+            )
 
         sent = []
 
@@ -145,8 +144,8 @@
         for stage in range(2):
             for i in (2, 0, 1):
                 for q in range(COLOURS):
-                    push(cast(q, STAGES[q][stage][i], core))
-                    push(cast(q, STAGES[q][stage][i], other))
+                    cast(q, STAGES[q][stage][i], core).start()
+                    cast(q, STAGES[q][stage][i], other).start()
         swaps = [
             pltpu.make_async_remote_copy(
                 src_ref=src, dst_ref=dst, send_sem=ex_s.at[i], recv_sem=ex_r.at[i],
@@ -187,8 +186,8 @@
             ctfv[...] = dot(hot, tabh[...], TN)
 
             def chunk(i, carry):
-                for t in range(width // LINE):
-                    at_ = pl.ds(pl.multiple_of(i * width + t * LINE, LINE), LINE)
+                for t in range(piece // LINE):
+                    at_ = pl.ds(pl.multiple_of(i * piece + t * LINE, LINE), LINE)
                     for p in range(16):
                         xs[t, 2 * p : 2 * p + 2, :] = xin[s, p, :, at_].astype(F32)
                     for part in range(2):
@@ -200,7 +199,7 @@
                             rbuf[pl.ds(r0, 16), at_] = (x * trigv[u : u + 1, at_]).astype(BF16)
                 return carry
 
-            lax.fori_loop(0, COLOURS, chunk, 0)
+            lax.fori_loop(0, CHUNKS, chunk, 0)
 
         for i in range(4):
             loads[i].wait()
@@ -208,10 +207,10 @@
         for i in range(3):
             for q in range(COLOURS):
                 k = STAGES[q][0][i]
-                for s in range(2):
-                    arrived(q, k, s)
-                    for t in STAGES[q][1][::-1]:
-                        push(relay(q, k, s, t))
+                settle(pbuf.at[k, :, :, :, span(q)], ag_s.at[0], ag_a.at[q, i]).wait_recv()
+                for t in STAGES[q][1][::-1]:
+                    for s in range(2):
+                        relay(q, k, s, t).start()
         spread_word(0)
         swaps[1].wait_recv()
         swaps[3].wait_recv()
@@ -237,6 +236,11 @@
         listed = jid == clane[0:1, :]
         for k in range(1, 8):
             listed = jnp.logical_or(listed, jid == clane[k : k + 1, :])
+        t32 = tabh[...].astype(F32)
+        ns32 = t32 * t32 * noisev[...]
+        ns_hi = ns32.astype(BF16)
+        nsv[0:BINS, :] = ns_hi
+        nsv[BINS : 2 * BINS, :] = (ns32 - ns_hi.astype(F32)).astype(BF16)
         bpscr[...] = jnp.zeros(bpscr.shape, F32)
         gscr[...] = jnp.zeros(gscr.shape, F32)
         spread_word(1)
@@ -250,14 +254,12 @@
             p32 = ps[0 : 8 * len(ks), :]
             nz = noisev[:, span(q)]
             got = dot((p32 * nz).astype(BF16), rbuf[:, span(q)], NT)
-            t32 = tabh[:, span(q)].astype(F32)
-            ns = t32 * t32 * nz
-            ns_hi = ns.astype(BF16)
-            ns_lo = (ns - ns_hi.astype(F32)).astype(BF16)
             pp = p32 * p32
             pp_hi = pp.astype(BF16)
             pp_lo = (pp - pp_hi.astype(F32)).astype(BF16)
-            power = dot(pp_hi, ns_hi, NT) + dot(pp_hi, ns_lo, NT) + dot(pp_lo, ns_hi, NT)
+            ns = nsv[:, span(q)]
+            power = dot(pp_hi, ns, NT)
+            power = power[:, 0:BINS] + power[:, BINS : 2 * BINS] + dot(pp_lo, ns[0:BINS], NT)
             for i, k in enumerate(ks):
                 here, there = slice(8 * i, 8 * i + 8), slice(8 * k, 8 * k + 8)
                 bpscr[there, 0:BINS] += power[here, :]
@@ -267,15 +269,11 @@
 
         swaps[0].wait_recv()
         for q in range(COLOURS):
-            for k in STAGES[q][1]:
-                for s in range(2):
-                    arrived(q, k, s)
+            settle(pbuf.at[1:4, :, :, :, span(q)], ag_s.at[0], ag_b.at[q]).wait_recv()
             score(q, (0,) + STAGES[q][0] + STAGES[q][1])
         for q in range(COLOURS):
             late = tuple(a ^ b for a in STAGES[q][0] for b in STAGES[q][1])
-            for k in late:
-                for s in range(2):
-                    arrived(q, k, s)
+            settle(pbuf.at[1:10, :, :, :, span(q)], ag_s.at[0], ag_l.at[q]).wait_recv()
             score(q, late)
         even, odd = pl.ds(0, 64, stride=2), pl.ds(1, 64, stride=2)
         ge = [gscr[k, even, :] for k in range(5)]
@@ -332,14 +330,16 @@
         def rs(q, k, t):
             return pltpu.make_async_remote_copy(
                 src_ref=dbuf.at[k, :, rspan(q)], dst_ref=rsb.at[k, :, rspan(q)],
-                send_sem=rs_s.at[q, k], recv_sem=rs_r.at[q, k],
+                send_sem=rs_s.at[0],
+                recv_sem=rs_b.at[q] if k == t else rs_a.at[q, STAGES[q][0].index(k ^ t)],
                 device_id=dev(t, core), device_id_type=MESH,
             )
 
         def collect(q, k, froms):
             acc = dbuf[k, :, rspan(q)].astype(F32)
+            arrival = rs_a.at[q, STAGES[q][0].index(k)] if k else rs_b.at[q]
+            settle(rsb.at[1 : 1 + len(froms), :, rspan(q)], rs_s.at[0], arrival).wait_recv()
             for child in froms:
-                rs(q, child, child ^ k).wait_recv()
                 acc = acc + rsb[child, :, rspan(q)].astype(F32)
             return acc
 
@@ -348,7 +348,7 @@
             dbuf[:, :, span(q)] = out.reshape(NODES, ROWS, width).astype(BF16)
             for k in STAGES[q][0] + (0,):
                 for t in STAGES[q][1][::-1]:
-                    push(rs(q, k ^ t, t))
+                    rs(q, k ^ t, t).start()
 
         lid = lax.broadcasted_iota(jnp.int32, (groups, lines), 0)
         tri = (
@@ -393,7 +393,7 @@
                 k = STAGES[q][0][i]
                 acc = collect(q, k, [k ^ t for t in STAGES[q][1]])
                 dbuf[k, :, rspan(q)] = acc.astype(BF16)
-                push(rs(q, k, k))
+                rs(q, k, k).start()
 
         def squares(i, carry):
             v = tabf[:, pl.ds(pl.multiple_of(i * LINE, LINE), LINE)].astype(F32)
@@ -423,19 +423,19 @@
 
         def wmsg(k):
             return pltpu.make_async_remote_copy(
-                src_ref=wzs, dst_ref=wzr.at[k], send_sem=w_s.at[k], recv_sem=w_r.at[k],
+                src_ref=wzs, dst_ref=wzr.at[k], send_sem=w_sem.at[0], recv_sem=w_sem.at[1],
                 device_id=((z + k) % groups, d), device_id_type=MESH,
             )
 
         def zmsg(k):
             return pltpu.make_async_remote_copy(
                 src_ref=zsend.at[(z + k) % groups, 0 : 4 * CAP], dst_ref=zrecv.at[k, 0 : 4 * CAP],
-                send_sem=z_s.at[k], recv_sem=z_r.at[k],
+                send_sem=z_sem.at[0], recv_sem=z_sem.at[1],
                 device_id=((z + k) % groups, d), device_id_type=MESH,
             )
 
         for k in order:
-            push(wmsg(k))
+            wmsg(k).start()
         zx.wait_recv()
         stack = jnp.concatenate(
             [
@@ -448,10 +448,10 @@
         packed = dot(sel[...], stack)
         zsend[...] = packed.astype(BF16).reshape(groups, slots, LINE)
         for k in order:
-            push(zmsg(k))
+            zmsg(k).start()
         acc_w = wzs[...]
+        settle(wzr.at[1:groups], w_sem.at[0], w_sem.at[1]).wait_recv()
         for k in range(1, groups):
-            wmsg(k).wait_recv()
             acc_w = acc_w + wzr[k]
         spread = (
             lax.broadcasted_iota(jnp.int32, (128, lines * BINS), 1) % BINS
@@ -466,16 +466,22 @@
         ok = wkey[...].astype(jnp.int32) == z * 8 + slot
         weights = dot(jnp.where(ok, coefw, 0.0), w3[...], NN, HIGH)
         for j in range(2):
-            o_weight[j] = weights[8 * j : 8 * j + CAP, :]
+            for c in range(CAP):
+                o_weight[c, j : j + 1, :] = weights[8 * j + c : 8 * j + c + 1, :]
         acc = zsend[z, 0 : 4 * CAP].astype(F32)
+        settle(zrecv.at[1:groups, 0 : 4 * CAP], z_sem.at[0], z_sem.at[1]).wait_recv()
         for k in range(1, groups):
-            zmsg(k).wait_recv()
             acc = acc + zrecv[k, 0 : 4 * CAP].astype(F32)
         for r in range(4):
-            o_data[r] = acc[CAP * r : CAP * r + CAP, :]
+            for c in range(CAP):
+                o_data[r // 2, c, r % 2 : r % 2 + 1, :] = acc[CAP * r + c : CAP * r + c + 1, :]
 
         for c in sent:
             c.wait_send()
+        settle(pbuf.at[1:NODES], ag_s.at[0], ag_l.at[0]).wait_send()
+        settle(dbuf.at[1:NODES], rs_s.at[0], rs_b.at[0]).wait_send()
+        settle(wzr.at[1:groups], w_sem.at[0], w_sem.at[1]).wait_send()
+        settle(zrecv.at[1:groups, 0 : 4 * CAP], z_sem.at[0], z_sem.at[1]).wait_send()
 
     return kernel
 
@@ -486,21 +492,21 @@
     lines = pixels // LINE
     half = pixels // 2
     trig = jnp.asarray(phase_rows(lines))
-    hbm = pl.BlockSpec(memory_space=pl.ANY)
+    hbm = pl.BlockSpec(memory_space=pltpu.HBM)
     vmem = pl.BlockSpec(memory_space=pltpu.VMEM)
     dma = pltpu.SemaphoreType.DMA
     data, weight = pl.pallas_call(
         make_kernel(lines, groups),
         name="estep",
         out_shape=(
-            jax.ShapeDtypeStruct((4, CAP, LINE), F32),
-            jax.ShapeDtypeStruct((2, CAP, LINE), F32),
+            jax.ShapeDtypeStruct((2, CAP, 2, LINE), F32),
+            jax.ShapeDtypeStruct((CAP, 2, LINE), F32),
         ),
         in_specs=[hbm] * 9,
         out_specs=(vmem, vmem),
         scratch_shapes=[
             pltpu.VMEM((2, 16, 2, half), BF16),
-            pltpu.VMEM((half // COLOURS // LINE, 32, LINE), F32),
+            pltpu.VMEM((half // CHUNKS // LINE, 32, LINE), F32),
             pltpu.VMEM((16, half), F32),
             pltpu.VMEM((2, 8, 16), jnp.int32),
             pltpu.VMEM((2, 1, 16), jnp.int32),
@@ -510,6 +516,7 @@
             pltpu.VMEM((BINS, half), BF16),
             pltpu.VMEM((BINS, pixels), BF16),
             pltpu.VMEM((1, half), F32),
+            pltpu.VMEM((2 * BINS, half), BF16),
             pltpu.VMEM((NODES, 2, 2, 2, half), BF16),
             pltpu.VMEM((128, half // COLOURS), F32),
             pltpu.VMEM((576, half), BF16),
@@ -529,9 +536,9 @@
             pltpu.VMEM((2, 128), F32),
             pltpu.VMEM((groups, 2, 128), F32),
             dma((10,)), dma((4,)), dma((4,)),
-            dma((4, 16, 2)), dma((4, 16, 2)), dma((4, 16)), dma((4, 16)),
-            dma((2,)), dma((2,)),
-            dma((groups,)), dma((groups,)), dma((groups,)), dma((groups,)),
+            dma((1,)), dma((COLOURS, 3)), dma((COLOURS,)), dma((COLOURS,)),
+            dma((1,)), dma((COLOURS, 3)), dma((COLOURS,)),
+            dma((2,)), dma((2,)), dma((2,)), dma((2,)),
             pltpu.SemaphoreType.REGULAR((3,)),
         ],
         compiler_params=pltpu.CompilerParams(
@@ -548,7 +555,7 @@
         line_slab,
         slab_owner.reshape(1, groups),
     )
-    return (data.reshape(1, 2, 2, CAP, LINE), weight[None])
+    return (jnp.transpose(data, (0, 2, 1, 3))[None], jnp.transpose(weight, (1, 0, 2))[None])
 
 
 def solution(mesh):

time: 56.1 us -> 52.3 us (0.932)
  Pallas kernels: 53.4 us -> 49.5 us
    pallas_call x1, Pallas kernels: 53.4 us -> 49.5 us  [body(): pl.pallas_call(make_kernel(lines, groups), name='estep', out_shape=(jax.S...]
where the time goes in v3:
time: 52.3 us; the launch traced here: 52.1 us
  Pallas kernels  49.5 us (95%)
  local copies, waits for them, and re-layouts  1.91 us (4%)
  between operations  0.65 us (1%)
    pallas_call x1, Pallas kernels, body(): pl.pallas_call(make_kernel(lines, groups), name='estep', out_shape=(jax.S...  49.5 us
    unnamed x4, local copies, waits for them, and re-layouts  1.91 us

profile of v3, /device:TPU:1, one launch (start us, length us, event | category | flops | bytes accessed | tf_op | source)
XLA Modules:
  0.0 52.1 jit_solution(9442024447341015905)
XLA Ops:
  0.6 49.5 %estep.1 = (f32[2,6,2,128]{3,2,1,0:T(2,128)}, f32[6,2,128]{2,1,0:T(2,128)}) custom-call(bf16[16,2,6144]{2,1,0:T(2,128)(2,1)} %parts.1, bf16[2,2,6144]{2,1,0:T(2,128)(2,1)} %proj.1, bf16[16,6144]{1,0:T(8,128)(2,1)} %table.1, f32[1,6144]{1,0:T(1,128)} %bitcast.10, f32[8,6144]{1,0:T(8,128)} %constant.2.clone.trig, s32[8,16]{1,0:T(8,128)} %bitcast.13, ...), custom_call_target="tpu_custom_call" | custom-call | tf_op jit(solution)/shard_map/estep/pallas_call | solution.py:498
  50.2 0.0 copy-start
  50.2 1.3 %copy.13 = f32[1,2,2,6,128]{4,2,3,1,0:T(2,128)} copy(f32[1,2,2,6,128]{4,2,3,1,0:T(2,128)} %bitcast.11) | data formatting | bytes 24576
  51.5 0.0 copy-done
  51.5 0.6 %copy.14 = f32[1,2,6,128]{3,1,2,0:T(2,128)} copy(f32[1,2,6,128]{3,1,2,0:T(2,128)S(1)} %bitcast.12) | data formatting | bytes 12288
Async XLA Ops:
  50.2 1.3 %copy-start = (f32[6,2,128]{2,1,0:T(2,128)S(1)}, f32[6,2,128]{2,1,0:T(2,128)}, u32[]{:S(2)}) copy-start(f32[6,2,128]{2,1,0:T(2,128)} %get-tuple-element.5) | copy-start | bytes 18436

commit v4 on v3

--- a/solution.py
+++ b/solution.py
@@ -64,7 +64,7 @@
                o_data, o_weight,
                xin, xs, ctfv, candb, binb, slabv, owners, trigv, tabh, tabf, noisev, nsv, pbuf, ps, rbuf,
                gscr, bpscr, sx, cscr, bsscr, dbuf, rsb, zb, sel, wkey, w3, zsend, zrecv, wzs, wzr,
-               loc, ex_s, ex_r, ag_s, ag_a, ag_b, ag_l, rs_s, rs_a, rs_b, sx_sem, zx_sem, z_sem, w_sem, ring):
+               loc, ex_s, ex_r, ag_s, ag_a, ag_b, ag_l, rs_s, rs_a, rs_b, sx_sem, zx_s, zx_r, z_sem, w_sem, ring):
         z = lax.axis_index("grp")
         d = lax.axis_index("dev")
         core = d % 2
@@ -211,7 +211,6 @@
                 for t in STAGES[q][1][::-1]:
                     for s in range(2):
                         relay(q, k, s, t).start()
-        spread_word(0)
         swaps[1].wait_recv()
         swaps[3].wait_recv()
         rotate(other)
@@ -243,7 +242,6 @@
         nsv[BINS : 2 * BINS, :] = (ns32 - ns_hi.astype(F32)).astype(BF16)
         bpscr[...] = jnp.zeros(bpscr.shape, F32)
         gscr[...] = jnp.zeros(gscr.shape, F32)
-        spread_word(1)
 
         def score(q, ks):
             for i, k in enumerate(ks):
@@ -271,6 +269,7 @@
         for q in range(COLOURS):
             settle(pbuf.at[1:4, :, :, :, span(q)], ag_s.at[0], ag_b.at[q]).wait_recv()
             score(q, (0,) + STAGES[q][0] + STAGES[q][1])
+        spread_word(0)
         for q in range(COLOURS):
             late = tuple(a ^ b for a in STAGES[q][0] for b in STAGES[q][1])
             settle(pbuf.at[1:10, :, :, :, span(q)], ag_s.at[0], ag_l.at[q]).wait_recv()
@@ -288,6 +287,7 @@
             device_id=mate, device_id_type=MESH,
         )
         push(trade)
+        spread_word(1)
         trade.wait_recv()
 
         last = sx[0, 2] + sx[1, 2]
@@ -318,11 +318,7 @@
         ):
             cscr[k, even, :] = a
             cscr[k, odd, :] = b
-        share = dot(both + zero, ohb, NT, HIGH)
-        bsscr[even, :] = share
-        bsscr[odd, :] = blank
         coef = jnp.concatenate([cscr[k] for k in range(5)], axis=1)[:, 0:576].astype(BF16)
-        dbuf[:, :, half : half + 128] = bsscr[...].reshape(NODES, ROWS, 128).astype(BF16)
 
         def rspan(q):
             return slice(q * width, (q + 1) * width + (128 if q == COLOURS - 1 else 0))
@@ -344,9 +340,14 @@
             return acc
 
         for q in range(COLOURS):
+            if q == COLOURS - 1:
+                share = dot(both + zero, ohb, NT, HIGH)
+                bsscr[even, :] = share
+                bsscr[odd, :] = blank
+                dbuf[:, :, half : half + 128] = bsscr[...].reshape(NODES, ROWS, 128).astype(BF16)
             out = dot(coef, rbuf[:, span(q)])
             dbuf[:, :, span(q)] = out.reshape(NODES, ROWS, width).astype(BF16)
-            for k in STAGES[q][0] + (0,):
+            for k in STAGES[q][0][::-1] + (0,):
                 for t in STAGES[q][1][::-1]:
                     rs(q, k ^ t, t).start()
 
@@ -355,10 +356,9 @@
             lax.broadcasted_iota(jnp.int32, (lines, lines), 0)
             < lax.broadcasted_iota(jnp.int32, (lines, lines), 1)
         ).astype(F32)
-        wide = (
-            lax.broadcasted_iota(jnp.int32, (lines, lines * ROWS), 1) // ROWS
-            == lax.broadcasted_iota(jnp.int32, (lines, lines * ROWS), 0)
-        ).astype(F32)
+        place = lax.broadcasted_iota(jnp.int32, (lines, lines * ROWS), 1) // ROWS
+        place = jnp.where(place < hl, place + core * hl, place - core * hl)
+        wide = (place == lax.broadcasted_iota(jnp.int32, (lines, lines * ROWS), 0)).astype(F32)
         wide16 = (
             lax.broadcasted_iota(jnp.int32, (lines, lines * BINS), 1) // BINS
             == lax.broadcasted_iota(jnp.int32, (lines, lines * BINS), 0)
@@ -388,7 +388,7 @@
         for j in range(2):
             wkey[8 * j : 8 * j + 8, :] = jnp.broadcast_to(dot(keys[j], wide16), (8, lines * BINS))
 
-        for i in range(3):
+        for i in (2, 1, 0):
             for q in range(COLOURS):
                 k = STAGES[q][0][i]
                 acc = collect(q, k, [k ^ t for t in STAGES[q][1]])
@@ -402,17 +402,19 @@
 
         lax.fori_loop(0, lines, squares, 0)
         spread_word(2)
+        def zx(q):
+            return pltpu.make_async_remote_copy(
+                src_ref=zb.at[core, :, span(q)], dst_ref=zb.at[core, :, span(q)],
+                send_sem=zx_s.at[q], recv_sem=zx_r.at[q], device_id=mate, device_id_type=MESH,
+            )
+
         extra = None
         for q in range(COLOURS):
             acc = collect(q, 0, STAGES[q][1] + STAGES[q][0])
             zb[core, :, span(q)] = acc[:, :width].astype(BF16)
+            push(zx(q))
             if q == COLOURS - 1:
                 extra = acc[:, width:]
-        zx = pltpu.make_async_remote_copy(
-            src_ref=zb.at[core], dst_ref=zb.at[core], send_sem=zx_sem.at[0], recv_sem=zx_sem.at[1],
-            device_id=mate, device_id_type=MESH,
-        )
-        push(zx)
 
         rows8 = lax.broadcasted_iota(jnp.int32, (8, 128), 0)
         for j in range(2):
@@ -436,16 +438,15 @@
 
         for k in order:
             wmsg(k).start()
-        zx.wait_recv()
-        stack = jnp.concatenate(
-            [
-                zb[h, :, LINE * i : LINE * i + LINE].astype(F32)
-                for h in range(2)
-                for i in range(hl)
-            ],
-            axis=0,
-        ).astype(BF16)
-        packed = dot(sel[...], stack)
+        def stack(h):
+            return jnp.concatenate(
+                [zb[h, :, LINE * i : LINE * i + LINE].astype(F32) for i in range(hl)], axis=0
+            ).astype(BF16)
+
+        packed = dot(sel[:, 0 : hl * ROWS], stack(core))
+        for q in range(COLOURS):
+            zx(q).wait_recv()
+        packed = packed + dot(sel[:, hl * ROWS :], stack(other))
         zsend[...] = packed.astype(BF16).reshape(groups, slots, LINE)
         for k in order:
             zmsg(k).start()
@@ -538,7 +539,7 @@
             dma((10,)), dma((4,)), dma((4,)),
             dma((1,)), dma((COLOURS, 3)), dma((COLOURS,)), dma((COLOURS,)),
             dma((1,)), dma((COLOURS, 3)), dma((COLOURS,)),
-            dma((2,)), dma((2,)), dma((2,)), dma((2,)),
+            dma((2,)), dma((COLOURS,)), dma((COLOURS,)), dma((2,)), dma((2,)),
             pltpu.SemaphoreType.REGULAR((3,)),
         ],
         compiler_params=pltpu.CompilerParams(

time: 52.3 us -> 49.9 us (0.954)
  Pallas kernels: 49.5 us -> 47.1 us
    pallas_call x1, Pallas kernels: 49.5 us -> 47.1 us  [body(): pl.pallas_call(make_kernel(lines, groups), name='estep', out_shape=(jax.S...]
where the time goes in v4:
time: 49.9 us; the launch traced here: 49.7 us
  Pallas kernels  47.1 us (94%)
  local copies, waits for them, and re-layouts  1.91 us (4%)
  between operations  0.65 us (1%)
    pallas_call x1, Pallas kernels, body(): pl.pallas_call(make_kernel(lines, groups), name='estep', out_shape=(jax.S...  47.1 us
    unnamed x4, local copies, waits for them, and re-layouts  1.91 us

profile of v4, /device:TPU:1, one launch (start us, length us, event | category | flops | bytes accessed | tf_op | source)
XLA Modules:
  0.0 49.7 jit_solution(18237684347475305951)
XLA Ops:
  0.6 47.1 %estep.1 = (f32[2,6,2,128]{3,2,1,0:T(2,128)}, f32[6,2,128]{2,1,0:T(2,128)}) custom-call(bf16[16,2,6144]{2,1,0:T(2,128)(2,1)} %parts.1, bf16[2,2,6144]{2,1,0:T(2,128)(2,1)} %proj.1, bf16[16,6144]{1,0:T(8,128)(2,1)} %table.1, f32[1,6144]{1,0:T(1,128)} %bitcast.10, f32[8,6144]{1,0:T(8,128)} %constant.2.clone.trig, s32[8,16]{1,0:T(8,128)} %bitcast.13, ...), custom_call_target="tpu_custom_call" | custom-call | tf_op jit(solution)/shard_map/estep/pallas_call | solution.py:499
  47.8 0.0 copy-start
  47.8 1.3 %copy.13 = f32[1,2,2,6,128]{4,2,3,1,0:T(2,128)} copy(f32[1,2,2,6,128]{4,2,3,1,0:T(2,128)} %bitcast.11) | data formatting | bytes 24576
  49.1 0.0 copy-done
  49.1 0.6 %copy.14 = f32[1,2,6,128]{3,1,2,0:T(2,128)} copy(f32[1,2,6,128]{3,1,2,0:T(2,128)S(1)} %bitcast.12) | data formatting | bytes 12288
Async XLA Ops:
  47.8 1.3 %copy-start = (f32[6,2,128]{2,1,0:T(2,128)S(1)}, f32[6,2,128]{2,1,0:T(2,128)}, u32[]{:S(2)}) copy-start(f32[6,2,128]{2,1,0:T(2,128)} %get-tuple-element.5) | copy-start | bytes 18436

commit v5 on v4

--- a/solution.py
+++ b/solution.py
@@ -142,7 +142,7 @@
             sent.append(c)
 
         for stage in range(2):
-            for i in (2, 0, 1):
+            for i in (0, 1, 2):
                 for q in range(COLOURS):
                     cast(q, STAGES[q][stage][i], core).start()
                     cast(q, STAGES[q][stage][i], other).start()

time: 49.9 us -> 49.6 us (level)
  no operation moved by 1% of the time
where the time goes in v5:
time: 49.6 us; the launch traced here: 49.5 us
  Pallas kernels  46.9 us (95%)
  local copies, waits for them, and re-layouts  1.91 us (4%)
  between operations  0.65 us (1%)
    pallas_call x1, Pallas kernels, body(): pl.pallas_call(make_kernel(lines, groups), name='estep', out_shape=(jax.S...  46.9 us
    unnamed x4, local copies, waits for them, and re-layouts  1.91 us

profile of v5, /device:TPU:1, one launch (start us, length us, event | category | flops | bytes accessed | tf_op | source)
XLA Modules:
  0.0 49.5 jit_solution(7897860257660031393)
XLA Ops:
  0.6 46.9 %estep.1 = (f32[2,6,2,128]{3,2,1,0:T(2,128)}, f32[6,2,128]{2,1,0:T(2,128)}) custom-call(bf16[16,2,6144]{2,1,0:T(2,128)(2,1)} %parts.1, bf16[2,2,6144]{2,1,0:T(2,128)(2,1)} %proj.1, bf16[16,6144]{1,0:T(8,128)(2,1)} %table.1, f32[1,6144]{1,0:T(1,128)} %bitcast.10, f32[8,6144]{1,0:T(8,128)} %constant.2.clone.trig, s32[8,16]{1,0:T(8,128)} %bitcast.13, ...), custom_call_target="tpu_custom_call" | custom-call | tf_op jit(solution)/shard_map/estep/pallas_call | solution.py:499
  47.6 0.0 copy-start
  47.6 1.3 %copy.13 = f32[1,2,2,6,128]{4,2,3,1,0:T(2,128)} copy(f32[1,2,2,6,128]{4,2,3,1,0:T(2,128)} %bitcast.11) | data formatting | bytes 24576
  48.9 0.0 copy-done
  48.9 0.6 %copy.14 = f32[1,2,6,128]{3,1,2,0:T(2,128)} copy(f32[1,2,6,128]{3,1,2,0:T(2,128)S(1)} %bitcast.12) | data formatting | bytes 12288
Async XLA Ops:
  47.6 1.3 %copy-start = (f32[6,2,128]{2,1,0:T(2,128)S(1)}, f32[6,2,128]{2,1,0:T(2,128)}, u32[]{:S(2)}) copy-start(f32[6,2,128]{2,1,0:T(2,128)} %get-tuple-element.5) | copy-start | bytes 18436

commit v6 on v5

--- a/solution.py
+++ b/solution.py
@@ -142,7 +142,7 @@
             sent.append(c)
 
         for stage in range(2):
-            for i in (0, 1, 2):
+            for i in (1, 0, 2):
                 for q in range(COLOURS):
                     cast(q, STAGES[q][stage][i], core).start()
                     cast(q, STAGES[q][stage][i], other).start()

time: 49.6 us -> 49.7 us (level)
  no operation moved by 1% of the time
where the time goes in v6:
time: 49.7 us; the launch traced here: 49.5 us
  Pallas kernels  47 us (95%)
  local copies, waits for them, and re-layouts  1.91 us (4%)
  between operations  0.65 us (1%)
    pallas_call x1, Pallas kernels, body(): pl.pallas_call(make_kernel(lines, groups), name='estep', out_shape=(jax.S...  47 us
    unnamed x4, local copies, waits for them, and re-layouts  1.91 us

profile of v6, /device:TPU:1, one launch (start us, length us, event | category | flops | bytes accessed | tf_op | source)
XLA Modules:
  0.0 49.5 jit_solution(11909917931041500832)
XLA Ops:
  0.6 47.0 %estep.1 = (f32[2,6,2,128]{3,2,1,0:T(2,128)}, f32[6,2,128]{2,1,0:T(2,128)}) custom-call(bf16[16,2,6144]{2,1,0:T(2,128)(2,1)} %parts.1, bf16[2,2,6144]{2,1,0:T(2,128)(2,1)} %proj.1, bf16[16,6144]{1,0:T(8,128)(2,1)} %table.1, f32[1,6144]{1,0:T(1,128)} %bitcast.10, f32[8,6144]{1,0:T(8,128)} %constant.2.clone.trig, s32[8,16]{1,0:T(8,128)} %bitcast.13, ...), custom_call_target="tpu_custom_call" | custom-call | tf_op jit(solution)/shard_map/estep/pallas_call | solution.py:499
  47.6 0.0 copy-start
  47.6 1.3 %copy.13 = f32[1,2,2,6,128]{4,2,3,1,0:T(2,128)} copy(f32[1,2,2,6,128]{4,2,3,1,0:T(2,128)} %bitcast.11) | data formatting | bytes 24576
  48.9 0.0 copy-done
  48.9 0.6 %copy.14 = f32[1,2,6,128]{3,1,2,0:T(2,128)} copy(f32[1,2,6,128]{3,1,2,0:T(2,128)S(1)} %bitcast.12) | data formatting | bytes 12288
Async XLA Ops:
  47.6 1.3 %copy-start = (f32[6,2,128]{2,1,0:T(2,128)S(1)}, f32[6,2,128]{2,1,0:T(2,128)}, u32[]{:S(2)}) copy-start(f32[6,2,128]{2,1,0:T(2,128)} %get-tuple-element.5) | copy-start | bytes 18436
